TPU v7x, 32 devices: a whole 2x2x4 slice. The times are simulated.
32 devices in a mesh: groups: 2 (over y), seq: 8 (over z, x), head: 2 (over core).
Axes of the slice: x: 2, y: 2, z: 4, core: 2. Of those that a mesh axis runs over, the one named last changes fastest.
Arguments:
- big_queries: bfloat16 [512, 4096], P(('groups', 'seq'), 'head'), parts along dimension 0, may hold values from -160 to 160
- big_keys: bfloat16 [512, 4096], P(('groups', 'seq'), 'head'), parts along dimension 0, may hold values from -8 to 8
- big_values: bfloat16 [512, 4096], P(('groups', 'seq'), 'head'), parts along dimension 0, may hold values from -6 to 6
- small_queries: bfloat16 [512, 1024], P(('groups', 'seq', 'head')), parts along dimension 0, may hold values from -160 to 160
- small_keys: bfloat16 [512, 1024], P(('groups', 'seq', 'head')), parts along dimension 0, may hold values from -8 to 8
- small_values: bfloat16 [512, 1024], P(('groups', 'seq', 'head')), parts along dimension 0, may hold values from -6 to 6
- big_readout: bfloat16 [4096, 64], P('head'), may hold values from -0.75 to 0.75
- small_readout: bfloat16 [1024, 64], replicated, may hold values from -1.5 to 1.5
- guidance: float32 [2], P('groups'), parts along dimension 0, may hold values from 1 to 4
Outputs:
- guided: float32 [256, 128], P(('groups', 'seq')), parts along dimension 0
There are 2 independent parts, one for each index of `groups`. A program takes and returns all parts, laid end to end along the dimension named above; an argument that names none is the same for every part. Nothing has to cross between parts.
All inputs are finite; a program needn't handle non-finite values.
Results may differ from a plain program's by a relative error of at most 0.0035.
Values may be sent and summed in bfloat16 or wider, within the bound.
A program may use at most 64 MiB of HBM per device.

v0:
```python
import functools
import math

import jax
import jax.numpy as jnp
from jax import lax
from jax.experimental import pallas as pl
from jax.experimental.pallas import tpu as pltpu
from jax.sharding import PartitionSpec as P

DH = 128


def split_heads(matrix, blocks, parts):
    rows_here, columns = matrix.shape
    shaped = matrix.reshape(blocks, rows_here // blocks, parts, columns // parts)
    shaped = jnp.transpose(shaped, (0, 2, 1, 3))
    return shaped.reshape(blocks * parts, rows_here // blocks, columns // parts)


def copy_heads(matrix, blocks, parts):
    rows_here, columns = matrix.shape
    shaped = jnp.transpose(matrix.reshape(rows_here, parts, columns // parts), (1, 0, 2))
    shaped = jnp.broadcast_to(shaped[None], (blocks, parts, rows_here, columns // parts))
    return shaped.reshape(blocks * parts, rows_here, columns // parts)


def join_heads(stacked, blocks, parts):
    pieces, rows_here, columns = stacked.shape
    shaped = stacked.reshape(blocks, parts, rows_here, columns)
    shaped = jnp.transpose(shaped, (0, 2, 1, 3))
    return shaped.reshape(blocks * rows_here, parts * columns)


def attend(query_rows, key_rows, value_rows):
    query_count = query_rows.shape[0]
    heads_here = query_rows.shape[1] // DH
    key_count = key_rows.shape[0]
    block_height = math.gcd(query_count, 256)
    block_count = query_count // block_height
    query_blocks = query_rows.reshape(block_count, block_height, heads_here, DH)
    key_split = key_rows.reshape(key_count, heads_here, DH)
    value_split = value_rows.reshape(key_count, heads_here, DH)
    score_scale = 1.0 / math.sqrt(DH)

    def one_block(query_block):
        scores = (
            jnp.einsum("qgd,kgd->gqk", query_block, key_split, preferred_element_type=jnp.float32)
            * score_scale
        )
        row_max = jnp.max(scores, axis=2, keepdims=True)
        probs = jnp.exp(scores - row_max)
        totals = jnp.sum(probs, axis=2, keepdims=True)
        weights = probs.astype(jnp.bfloat16)
        accumulated = jnp.einsum(
            "gqk,kgd->gqd", weights, value_split, preferred_element_type=jnp.float32
        )
        attended = accumulated / totals
        attended = jnp.transpose(attended, (1, 0, 2)).reshape(block_height, heads_here * DH)
        return attended.astype(jnp.bfloat16)

    outputs = lax.map(one_block, query_blocks)
    return outputs.reshape(query_count, heads_here * DH)


def exchanged(
    big_queries,
    big_keys,
    big_values,
    small_queries,
    small_keys,
    small_values,
    big_readout,
    small_readout,
    guidance,
):
    seq_count = lax.axis_size("seq")
    big_heads = big_queries.shape[1] // DH
    big_group = max(big_heads // seq_count, 1)
    big_blocks = max(seq_count // big_heads, 1)
    big_parts = big_heads // big_group
    query_rows = lax.all_to_all(
        split_heads(big_queries, big_blocks, big_parts),
        "seq",
        split_axis=0,
        concat_axis=1,
        tiled=True,
    )[0]
    key_copies, value_copies = (
        lax.all_to_all(
            copy_heads(big_keys, big_blocks, big_parts),
            "seq",
            split_axis=0,
            concat_axis=1,
            tiled=True,
        ),
        lax.all_to_all(
            copy_heads(big_values, big_blocks, big_parts),
            "seq",
            split_axis=0,
            concat_axis=1,
            tiled=True,
        ),
    )
    key_rows = key_copies[0]
    value_rows = value_copies[0]
    big_out = attend(query_rows, key_rows, value_rows)
    big_back = lax.all_to_all(big_out[None], "seq", split_axis=1, concat_axis=0, tiled=True)
    big_attention = join_heads(big_back, big_blocks, big_parts)
    big_partial = jnp.dot(big_attention, big_readout, preferred_element_type=jnp.float32)
    small_heads = small_queries.shape[1] // DH
    small_group = max(small_heads // seq_count, 1)
    small_blocks = max(seq_count // small_heads, 1)
    small_parts = small_heads // small_group
    small_query_rows = lax.all_to_all(
        split_heads(small_queries, small_blocks, small_parts),
        "seq",
        split_axis=0,
        concat_axis=1,
        tiled=True,
    )[0]
    key_copies, value_copies = (
        lax.all_to_all(
            copy_heads(small_keys, small_blocks, small_parts),
            "seq",
            split_axis=0,
            concat_axis=1,
            tiled=True,
        ),
        lax.all_to_all(
            copy_heads(small_values, small_blocks, small_parts),
            "seq",
            split_axis=0,
            concat_axis=1,
            tiled=True,
        ),
    )
    small_key_rows, small_value_rows = (
        lax.all_gather(key_copies[0], "head", axis=0, tiled=True),
        lax.all_gather(value_copies[0], "head", axis=0, tiled=True),
    )
    small_out = attend(small_query_rows, small_key_rows, small_value_rows)
    small_back = lax.all_to_all(small_out[None], "seq", split_axis=1, concat_axis=0, tiled=True)
    small_attention = join_heads(small_back, small_blocks, small_parts)
    small_latent = jnp.dot(small_attention, small_readout, preferred_element_type=jnp.float32)
    weight_value = guidance[0]
    core_index = lax.axis_index("head")
    placed = lax.dynamic_update_slice(
        jnp.zeros_like(big_partial),
        small_latent,
        (core_index * small_latent.shape[0], jnp.zeros((), jnp.int32)),
    )
    blended = lax.psum((1.0 + weight_value) * big_partial - weight_value * placed, "head")
    return blended.reshape(blended.shape[0] // 2, 2 * blended.shape[1])


MESH = pl.DeviceIdType.MESH


def far_first(count):
    return sorted(range(1, count), key=lambda offset: -min(offset, count - offset))


def softmax_parts(query_head, key_head):
    scores = lax.dot_general(
        query_head, key_head, (((1,), (1,)), ((), ())), preferred_element_type=jnp.float32
    ) * (1.0 / math.sqrt(DH))
    row_max = jnp.max(scores, axis=1, keepdims=True)
    probs = jnp.exp(scores - row_max)
    totals = jnp.sum(probs, axis=1, keepdims=True)
    return probs.astype(jnp.bfloat16), totals


def weigh(weights, totals, value_head):
    accumulated = jnp.dot(weights, value_head, preferred_element_type=jnp.float32)
    return (accumulated / totals).astype(jnp.bfloat16)


def fused_kernel(
    n,
    m,
    guidance,
    big_q,
    big_k,
    big_v,
    small_q,
    small_k,
    small_v,
    big_read,
    small_read,
    out,
    all_q,
    all_k,
    all_v,
    few_q,
    few_k,
    few_v,
    read_big,
    read_small,
    weights,
    latent,
    small_part,
    stage,
    arrived,
    guide,
    own_sem,
    big_send,
    big_recv,
    small_send,
    small_recv,
    back_send,
    back_recv,
):
    group = lax.axis_index("groups")
    me = lax.axis_index("seq")
    core = lax.axis_index("head")
    rows = big_q.shape[0]
    width = all_q.shape[1]
    few_rows = small_q.shape[0]
    few_width = few_q.shape[1]
    heads_here = width // DH
    few_heads = few_width // DH
    lat = big_read.shape[0]
    half = stage.shape[1]
    order = far_first(n)

    def ahead(offset):
        return lax.rem(me + offset, n)

    def behind(offset):
        return lax.rem(me + n - offset, n)

    def window(ref, index, size):
        return ref.at[:, pl.ds(pl.multiple_of(index * size, size), size)]

    def big_land(ref, seq):
        return ref.at[pl.ds(pl.multiple_of(seq * rows, rows), rows), :]

    def few_land(ref, seq, which):
        start = pl.multiple_of((seq * m + which) * few_rows, few_rows)
        return ref.at[pl.ds(start, few_rows), :]

    big_pairs = ((big_k, all_k), (big_q, all_q), (big_v, all_v))
    few_pairs = ((small_k, few_k), (small_q, few_q), (small_v, few_v))

    def big_copy(item, offset, landing):
        source, target = big_pairs[item]
        peer = ahead(offset)
        return pltpu.make_async_remote_copy(
            src_ref=window(source, peer, width),
            dst_ref=big_land(target, landing),
            send_sem=big_send.at[item, offset],
            recv_sem=big_recv.at[item, offset],
            device_id=(group, peer, core),
            device_id_type=MESH,
        )

    def few_copy(item, offset, landing, which):
        source, target = few_pairs[item]
        peer = ahead(offset)
        return pltpu.make_async_remote_copy(
            src_ref=window(source, peer, few_width),
            dst_ref=few_land(target, landing, which),
            send_sem=small_send.at[item, offset],
            recv_sem=small_recv.at[item, offset, which],
            device_id=(group, peer, 0),
            device_id_type=MESH,
        )

    def back_copy(offset, turn, slot_core):
        peer = ahead(offset)
        return pltpu.make_async_remote_copy(
            src_ref=stage.at[peer],
            dst_ref=arrived.at[offset, slot_core],
            send_sem=back_send.at[offset, turn],
            recv_sem=back_recv.at[offset, slot_core],
            device_id=(group, peer, lax.rem(core + turn, m)),
            device_id_type=MESH,
        )

    barrier = pltpu.get_barrier_semaphore()
    for offset in range(n):
        for turn in range(m):
            if offset or turn:
                pl.semaphore_signal(
                    barrier,
                    inc=1,
                    device_id=(group, ahead(offset), lax.rem(core + turn, m)),
                    device_id_type=MESH,
                )

    read_rows = pl.ds(pl.multiple_of(me * width, width), width)
    few_read_rows = pl.ds(pl.multiple_of(me * few_width, few_width), few_width)
    own = [
        pltpu.make_async_copy(
            window(source, me, width), big_land(target, me), own_sem.at[item]
        )
        for item, (source, target) in enumerate(big_pairs)
    ]
    own.append(pltpu.make_async_copy(big_read.at[:, read_rows], read_big, own_sem.at[3]))
    own.append(
        pltpu.make_async_copy(small_read.at[:, few_read_rows], read_small, own_sem.at[4])
    )
    own.append(pltpu.make_async_copy(guidance, guide, own_sem.at[8]))
    few_own = [
        pltpu.make_async_copy(
            window(source, me, few_width), few_land(target, me, 0), own_sem.at[5 + item]
        )
        for item, (source, target) in enumerate(few_pairs)
    ]
    for copy in own:
        copy.start()

    @pl.when(core == 0)
    def _():
        for copy in few_own:
            copy.start()

    pl.semaphore_wait(barrier, n * m - 1)

    for offset in order:
        for item in range(3):
            few_copy(item, offset, me, core).start()

    @pl.when(core != 0)
    def _():
        for item in range(3):
            few_copy(item, 0, me, core).start()

    for items in ((0, 1), (2,)):
        for offset in order:
            for item in items:
                big_copy(item, offset, me).start()

    for copy in own:
        copy.wait()
    weight_value = guide[0]
    lanes = lax.broadcasted_iota(jnp.int32, (latent.shape[0] // 2, 2 * lat), 1)

    def paired(attended, readout):
        doubled = jnp.concatenate([readout, readout], axis=0)
        latent[...] = lax.dot_general(
            attended, doubled, (((1,), (1,)), ((), ())), preferred_element_type=jnp.float32
        )
        even = latent[pl.ds(0, latent.shape[0] // 2, stride=2), :]
        odd = latent[pl.ds(1, latent.shape[0] // 2, stride=2), :]
        return jnp.where(lanes < lat, even, odd)

    @pl.when(core == 0)
    def _():
        for copy in few_own:
            copy.wait()
        for which in range(m):
            for offset in range(n):
                if offset or which:
                    for item in range(3):
                        few_copy(item, offset, behind(offset), which).wait_recv()
        pieces = []
        for head in range(few_heads):
            columns = slice(head * DH, (head + 1) * DH)
            probs, totals = softmax_parts(few_q[:, columns], few_k[:, columns])
            pieces.append(weigh(probs, totals, few_v[:, columns]))
        attended = pieces[0] if few_heads == 1 else jnp.concatenate(pieces, axis=1)
        small_part[...] = weight_value * paired(attended, read_small[...])

    @pl.when(core != 0)
    def _():
        small_part[...] = jnp.zeros_like(small_part)

    for offset in order:
        for item in (0, 1):
            big_copy(item, offset, behind(offset)).wait_recv()
    totals_of = []
    for head in range(heads_here):
        columns = slice(head * DH, (head + 1) * DH)
        probs, totals = softmax_parts(all_q[:, columns], all_k[:, columns])
        weights[head] = probs
        totals_of.append(totals)
    for offset in order:
        big_copy(2, offset, behind(offset)).wait_recv()
    pieces = [
        weigh(weights[head], totals_of[head], all_v[:, head * DH : (head + 1) * DH])
        for head in range(heads_here)
    ]
    attended = pieces[0] if heads_here == 1 else jnp.concatenate(pieces, axis=1)
    term = (1.0 + weight_value) * paired(attended, read_big[...]) - small_part[...]
    stage[...] = term.reshape(n, half, 2 * lat)
    arrived[0, core] = stage[me]

    for offset in order + [0]:
        for turn in range(m):
            if offset or turn:
                back_copy(offset, turn, core).start()
    for offset in range(n):
        for slot_core in range(m):
            if offset:
                back_copy(offset, 0, slot_core).wait_recv()
    for turn in range(1, m):
        back_copy(0, turn, lax.rem(core + turn, m)).wait_recv()
    out[...] = jnp.sum(arrived[...].reshape(n * m, half, 2 * lat), axis=0)

    for offset in order:
        for item in range(3):
            few_copy(item, offset, me, core).wait_send()
            big_copy(item, offset, me).wait_send()

    @pl.when(core != 0)
    def _():
        for item in range(3):
            few_copy(item, 0, me, core).wait_send()

    for offset in order + [0]:
        for turn in range(m):
            if offset or turn:
                back_copy(offset, turn, core).wait_send()


def fused(
    n,
    m,
    big_queries,
    big_keys,
    big_values,
    small_queries,
    small_keys,
    small_values,
    big_readout,
    small_readout,
    guidance,
):
    rows, columns = big_queries.shape
    few_rows, few_columns = small_queries.shape
    width, few_width = columns // n, few_columns // n
    tokens = rows * n
    lat = big_readout.shape[1]
    half = rows // 2
    kind = jnp.bfloat16
    dma = pltpu.SemaphoreType.DMA
    return pl.pallas_call(
        functools.partial(fused_kernel, n, m),
        out_shape=pltpu.VMEM((half, 2 * lat), jnp.float32),
        in_specs=[pl.BlockSpec(memory_space=pl.ANY)] * 9,
        out_specs=pl.BlockSpec(memory_space=pltpu.VMEM),
        scratch_shapes=[
            pltpu.VMEM((tokens, width), kind),
            pltpu.VMEM((tokens, width), kind),
            pltpu.VMEM((tokens, width), kind),
            pltpu.VMEM((tokens, few_width), kind),
            pltpu.VMEM((tokens, few_width), kind),
            pltpu.VMEM((tokens, few_width), kind),
            pltpu.VMEM((lat, width), kind),
            pltpu.VMEM((lat, few_width), kind),
            pltpu.VMEM((width // DH, tokens, tokens), kind),
            pltpu.VMEM((tokens, 2 * lat), jnp.float32),
            pltpu.VMEM((tokens // 2, 2 * lat), jnp.float32),
            pltpu.VMEM((n, half, 2 * lat), jnp.float32),
            pltpu.VMEM((n, m, half, 2 * lat), jnp.float32),
            pltpu.SMEM((1,), jnp.float32),
            dma((9,)),
            dma((3, n)),
            dma((3, n)),
            dma((3, n)),
            dma((3, n, m)),
            dma((n, m)),
            dma((n, m)),
        ],
        compiler_params=pltpu.CompilerParams(collective_id=0, has_side_effects=True),
        name="fused_window",
    )(
        guidance,
        big_queries,
        big_keys,
        big_values,
        small_queries,
        small_keys,
        small_values,
        big_readout.T,
        small_readout.T,
    )


def fits(n, m, big_queries, small_queries, lat):
    rows, columns = big_queries.shape
    few_rows, few_columns = small_queries.shape
    return (
        n > 1
        and m > 1
        and n * rows <= 512
        and columns % (n * DH) == 0
        and few_columns % (n * DH) == 0
        and rows == m * few_rows
        and few_rows % 16 == 0
        and 2 * lat == 128
    )


def shards(*arguments):
    n, m = lax.axis_size("seq"), lax.axis_size("head")
    if fits(n, m, arguments[0], arguments[3], arguments[6].shape[1]):
        return fused(n, m, *arguments)
    return exchanged(*arguments)


def solution(mesh):
    placed = (
        P(("groups", "seq"), "head"),
        P(("groups", "seq"), "head"),
        P(("groups", "seq"), "head"),
        P(("groups", "seq", "head"), None),
        P(("groups", "seq", "head"), None),
        P(("groups", "seq", "head"), None),
        P("head", None),
        P(),
        P("groups"),
    )
    return jax.shard_map(
        shards, mesh=mesh, in_specs=placed, out_specs=P(("groups", "seq"), None), check_vma=False
    )
```

profile of v0, /device:TPU:0, one launch (start us, length us, event | category | flops | bytes accessed | tf_op | source)
XLA Modules:
  0.0 27.2 jit_solution(100536839201472979)
XLA Ops:
  0.7 25.9 %fused_window.1 = f32[16,128]{1,0:T(8,128)S(1)} custom-call(f32[1]{0:T(128)S(6)} %copy.12.guidance, bf16[32,2048]{1,0:T(8,128)(2,1)} %big_q.1, bf16[32,2048]{1,0:T(8,128)(2,1)} %big_k.1, bf16[32,2048]{1,0:T(8,128)(2,1)} %big_v.1, bf16[16,1024]{1,0:T(8,128)(2,1)} %small_q.1, bf16[16,1024]{1,0:T(8,128)(2,1)} %small_k.1, bf16[16,1024]{1,0:T(8,128)(2,1)} %small_v.1, ...), custom_call_target="tpu_custom_call" | custom-call | tf_op jit(solution)/shard_map/fused_window/pallas_call | solution.py:439
  26.6 0.6 %copy.11 = f32[16,128]{1,0:T(8,128)} copy(f32[16,128]{1,0:T(8,128)S(1)} %fused_window.1) | data formatting | bytes 16384
where the time goes:
time: 27.3 us; the launch traced here: 27.2 us
  Pallas kernels  25.9 us (95%)
  between operations  0.66 us (2%)
  local copies, waits for them, and re-layouts  0.6 us (2%)
    pallas_call x1, Pallas kernels, fused(): pl.pallas_call(functools.partial(fused_kernel, n, m), out_shape=pltpu.VME...  25.9 us
    unnamed x1, local copies, waits for them, and re-layouts  0.6 us

commit v1 on v0

--- a/solution.py
+++ b/solution.py
@@ -157,10 +157,6 @@
 MESH = pl.DeviceIdType.MESH
 
 
-def far_first(count):
-    return sorted(range(1, count), key=lambda offset: -min(offset, count - offset))
-
-
 def softmax_parts(query_head, key_head):
     scores = lax.dot_general(
         query_head, key_head, (((1,), (1,)), ((), ())), preferred_element_type=jnp.float32
@@ -171,12 +167,13 @@
     return probs.astype(jnp.bfloat16), totals
 
 
-def weigh(weights, totals, value_head):
-    accumulated = jnp.dot(weights, value_head, preferred_element_type=jnp.float32)
-    return (accumulated / totals).astype(jnp.bfloat16)
-
-
-def fused_kernel(
+def read_out(values, readout):
+    return lax.dot_general(
+        values, readout, (((1,), (1,)), ((), ())), preferred_element_type=jnp.float32
+    )
+
+
+def window_kernel(
     n,
     m,
     guidance,
@@ -191,38 +188,51 @@
     out,
     all_q,
     all_k,
-    all_v,
+    all_w,
     few_q,
     few_k,
-    few_v,
+    few_w,
+    own_v,
+    own_few_v,
     read_big,
     read_small,
+    ready_w,
+    half_w,
+    other_w,
+    ready_few,
     weights,
+    small_part,
     latent,
-    small_part,
     stage,
     arrived,
+    swap,
     guide,
+    near,
     own_sem,
     big_send,
     big_recv,
     small_send,
     small_recv,
+    few_send,
+    few_recv,
+    core_sem,
     back_send,
     back_recv,
+    swap_sem,
 ):
     group = lax.axis_index("groups")
     me = lax.axis_index("seq")
     core = lax.axis_index("head")
+    rungs = n // 2
+    rung, side = lax.div(me, 2), lax.rem(me, 2)
     rows = big_q.shape[0]
     width = all_q.shape[1]
     few_rows = small_q.shape[0]
     few_width = few_q.shape[1]
     heads_here = width // DH
-    few_heads = few_width // DH
     lat = big_read.shape[0]
-    half = stage.shape[1]
-    order = far_first(n)
+    half = rows // 2
+    part = half // m
 
     def ahead(offset):
         return lax.rem(me + offset, n)
@@ -230,85 +240,141 @@
     def behind(offset):
         return lax.rem(me + n - offset, n)
 
+    def offset_to(peer):
+        return lax.rem(peer - me + n, n)
+
     def window(ref, index, size):
         return ref.at[:, pl.ds(pl.multiple_of(index * size, size), size)]
 
-    def big_land(ref, seq):
-        return ref.at[pl.ds(pl.multiple_of(seq * rows, rows), rows), :]
-
-    def few_land(ref, seq, which):
-        start = pl.multiple_of((seq * m + which) * few_rows, few_rows)
-        return ref.at[pl.ds(start, few_rows), :]
-
-    big_pairs = ((big_k, all_k), (big_q, all_q), (big_v, all_v))
-    few_pairs = ((small_k, few_k), (small_q, few_q), (small_v, few_v))
-
-    def big_copy(item, offset, landing):
-        source, target = big_pairs[item]
-        peer = ahead(offset)
+    def row_block(ref, index, size):
+        return ref.at[pl.ds(pl.multiple_of(index * size, size), size), :]
+
+    def toward(distance, act):
+        for up in range(rungs - 1, -rungs, -1):
+            across = distance - abs(up)
+            if across not in (0, 1):
+                continue
+            peer = (rung + up) * 2 + lax.rem(side + across, 2)
+            if up == 0:
+                act(peer)
+            elif up > 0:
+                pl.when(rung + up < rungs)(functools.partial(act, peer))
+            else:
+                pl.when(rung + up >= 0)(functools.partial(act, peer))
+
+    def key_rows(seq, which):
+        return which * n + seq
+
+    def query_rows(seq, which):
+        return seq * m + which
+
+    big_pairs = ((big_k, all_k), (big_q, all_q))
+    few_pairs = ((small_k, few_k, key_rows), (small_q, few_q, query_rows))
+
+    def big_copy(item, peer, offset):
+        if item == 2:
+            source, target = ready_w.at[peer], all_w
+        else:
+            source, target = window(big_pairs[item][0], peer, width), big_pairs[item][1]
         return pltpu.make_async_remote_copy(
-            src_ref=window(source, peer, width),
-            dst_ref=big_land(target, landing),
+            src_ref=source,
+            dst_ref=row_block(target, me, rows),
             send_sem=big_send.at[item, offset],
             recv_sem=big_recv.at[item, offset],
             device_id=(group, peer, core),
             device_id_type=MESH,
         )
 
-    def few_copy(item, offset, landing, which):
-        source, target = few_pairs[item]
-        peer = ahead(offset)
+    def few_copy(item, peer, offset, which):
+        source, target, place = few_pairs[item]
         return pltpu.make_async_remote_copy(
             src_ref=window(source, peer, few_width),
-            dst_ref=few_land(target, landing, which),
+            dst_ref=row_block(target, place(me, which), few_rows),
             send_sem=small_send.at[item, offset],
             recv_sem=small_recv.at[item, offset, which],
             device_id=(group, peer, 0),
             device_id_type=MESH,
         )
 
-    def back_copy(offset, turn, slot_core):
-        peer = ahead(offset)
+    def few_w_copy(peer, offset):
         return pltpu.make_async_remote_copy(
-            src_ref=stage.at[peer],
+            src_ref=ready_few.at[peer],
+            dst_ref=row_block(few_w, me, few_rows),
+            send_sem=few_send.at[offset],
+            recv_sem=few_recv.at[offset],
+            device_id=(group, peer, 0),
+            device_id_type=MESH,
+        )
+
+    def core_copy():
+        return pltpu.make_async_remote_copy(
+            src_ref=half_w,
+            dst_ref=other_w,
+            send_sem=core_sem.at[0],
+            recv_sem=core_sem.at[1],
+            device_id=(group, me, 0),
+            device_id_type=MESH,
+        )
+
+    def back_copy(peer, offset, turn, slot_core):
+        target_core = lax.rem(core + turn, m)
+        return pltpu.make_async_remote_copy(
+            src_ref=stage.at[peer, target_core],
             dst_ref=arrived.at[offset, slot_core],
             send_sem=back_send.at[offset, turn],
             recv_sem=back_recv.at[offset, slot_core],
-            device_id=(group, peer, lax.rem(core + turn, m)),
+            device_id=(group, peer, target_core),
             device_id_type=MESH,
         )
 
+    def swap_copy():
+        return pltpu.make_async_remote_copy(
+            src_ref=swap.at[0],
+            dst_ref=swap.at[1],
+            send_sem=swap_sem.at[0],
+            recv_sem=swap_sem.at[1],
+            device_id=(group, me, 1 - core),
+            device_id_type=MESH,
+        )
+
     barrier = pltpu.get_barrier_semaphore()
-    for offset in range(n):
-        for turn in range(m):
-            if offset or turn:
-                pl.semaphore_signal(
-                    barrier,
-                    inc=1,
-                    device_id=(group, ahead(offset), lax.rem(core + turn, m)),
-                    device_id_type=MESH,
-                )
-
-    read_rows = pl.ds(pl.multiple_of(me * width, width), width)
-    few_read_rows = pl.ds(pl.multiple_of(me * few_width, few_width), few_width)
+    neighbours = (
+        1 + (rung > 0).astype(jnp.int32) + (rung < rungs - 1).astype(jnp.int32)
+    )
+
+    def greet(peer):
+        for which in range(m):
+            pl.semaphore_signal(
+                barrier, inc=1, device_id=(group, peer, which), device_id_type=MESH
+            )
+
+    toward(1, greet)
+    pl.semaphore_signal(
+        barrier, inc=1, device_id=(group, me, 1 - core), device_id_type=MESH
+    )
+
+    value_copies = [
+        pltpu.make_async_copy(big_v, own_v, own_sem.at[0]),
+        pltpu.make_async_copy(big_read, read_big, own_sem.at[1]),
+        pltpu.make_async_copy(small_v, own_few_v, own_sem.at[2]),
+        pltpu.make_async_copy(small_read, read_small, own_sem.at[3]),
+    ]
     own = [
         pltpu.make_async_copy(
-            window(source, me, width), big_land(target, me), own_sem.at[item]
+            window(source, me, width), row_block(target, me, rows), own_sem.at[4 + item]
         )
         for item, (source, target) in enumerate(big_pairs)
     ]
-    own.append(pltpu.make_async_copy(big_read.at[:, read_rows], read_big, own_sem.at[3]))
-    own.append(
-        pltpu.make_async_copy(small_read.at[:, few_read_rows], read_small, own_sem.at[4])
-    )
-    own.append(pltpu.make_async_copy(guidance, guide, own_sem.at[8]))
+    own.append(pltpu.make_async_copy(guidance, guide, own_sem.at[6]))
     few_own = [
         pltpu.make_async_copy(
-            window(source, me, few_width), few_land(target, me, 0), own_sem.at[5 + item]
-        )
-        for item, (source, target) in enumerate(few_pairs)
+            window(source, me, few_width),
+            row_block(target, place(me, 0), few_rows),
+            own_sem.at[7 + item],
+        )
+        for item, (source, target, place) in enumerate(few_pairs)
     ]
-    for copy in own:
+    for copy in value_copies + own:
         copy.start()
 
     @pl.when(core == 0)
@@ -316,103 +382,168 @@
         for copy in few_own:
             copy.start()
 
-    pl.semaphore_wait(barrier, n * m - 1)
-
-    for offset in order:
-        for item in range(3):
-            few_copy(item, offset, me, core).start()
+    def start_scores(peer):
+        offset = offset_to(peer)
+        for item in (0, 1):
+            few_copy(item, peer, offset, core).start()
+        for item in (0, 1):
+            big_copy(item, peer, offset).start()
+
+    def pass_on(round_index):
+        def act(peer):
+            pl.semaphore_signal(
+                near.at[round_index], inc=1, device_id=(group, peer, core), device_id_type=MESH
+            )
+
+        return act
+
+    pl.semaphore_wait(barrier, m * neighbours + 1)
+    toward(1, pass_on(0))
+    toward(1, start_scores)
 
     @pl.when(core != 0)
     def _():
-        for item in range(3):
-            few_copy(item, 0, me, core).start()
-
-    for items in ((0, 1), (2,)):
-        for offset in order:
-            for item in items:
-                big_copy(item, offset, me).start()
+        for item in (0, 1):
+            few_copy(item, me, 0, core).start()
+
+    for copy in value_copies:
+        copy.wait()
+    few_lanes = lax.broadcasted_iota(jnp.int32, (few_rows, 2 * lat), 1)
+    for seq in range(n):
+        columns = slice(seq * few_width, (seq + 1) * few_width)
+        term = read_out(own_few_v[:, columns], read_small[:, columns])
+        both = jnp.concatenate([term, term], axis=1)
+        mine = (few_lanes < lat) == (core == 0)
+        half_w[seq] = jnp.where(mine, both, 0.0).astype(half_w.dtype)
+
+    @pl.when(core != 0)
+    def _():
+        core_copy().start()
+
+    for seq in range(n):
+        terms = []
+        for head in range(heads_here):
+            columns = slice(seq * width + head * DH, seq * width + (head + 1) * DH)
+            terms.append(read_out(own_v[:, columns], read_big[:, columns]))
+        ready_w[seq] = jnp.concatenate(terms, axis=1).astype(ready_w.dtype)
+
+    for distance in range(2, rungs + 1):
+        pl.semaphore_wait(near.at[distance - 2], neighbours)
+        if distance < rungs:
+            toward(1, pass_on(distance - 1))
+        toward(distance, start_scores)
+
+    @pl.when(core == 0)
+    def _():
+        core_copy().wait_recv()
+        ready_few[...] = half_w[...] + other_w[...]
+        for distance in range(rungs, 0, -1):
+            toward(distance, lambda peer: few_w_copy(peer, offset_to(peer)).start())
+        few_w[pl.ds(pl.multiple_of(me * few_rows, few_rows), few_rows), :] = ready_few[me]
+
+    for distance in range(rungs, 0, -1):
+        toward(distance, lambda peer: big_copy(2, peer, offset_to(peer)).start())
+    all_w[pl.ds(pl.multiple_of(me * rows, rows), rows), :] = ready_w[me]
 
     for copy in own:
         copy.wait()
     weight_value = guide[0]
-    lanes = lax.broadcasted_iota(jnp.int32, (latent.shape[0] // 2, 2 * lat), 1)
-
-    def paired(attended, readout):
-        doubled = jnp.concatenate([readout, readout], axis=0)
-        latent[...] = lax.dot_general(
-            attended, doubled, (((1,), (1,)), ((), ())), preferred_element_type=jnp.float32
-        )
-        even = latent[pl.ds(0, latent.shape[0] // 2, stride=2), :]
-        odd = latent[pl.ds(1, latent.shape[0] // 2, stride=2), :]
-        return jnp.where(lanes < lat, even, odd)
+    lanes = lax.broadcasted_iota(jnp.int32, latent.shape, 1)
 
     @pl.when(core == 0)
     def _():
         for copy in few_own:
             copy.wait()
-        for which in range(m):
-            for offset in range(n):
+        for offset in range(n):
+            for which in range(m):
                 if offset or which:
-                    for item in range(3):
-                        few_copy(item, offset, behind(offset), which).wait_recv()
-        pieces = []
-        for head in range(few_heads):
-            columns = slice(head * DH, (head + 1) * DH)
-            probs, totals = softmax_parts(few_q[:, columns], few_k[:, columns])
-            pieces.append(weigh(probs, totals, few_v[:, columns]))
-        attended = pieces[0] if few_heads == 1 else jnp.concatenate(pieces, axis=1)
-        small_part[...] = weight_value * paired(attended, read_small[...])
+                    for item in (0, 1):
+                        few_copy(item, behind(offset), offset, which).wait_recv()
+        probs, totals = softmax_parts(few_q[...], few_k[...])
+        for offset in range(1, n):
+            few_w_copy(behind(offset), offset).wait_recv()
+        keys = n * few_rows
+        held = few_w[...]
+        terms = [
+            jnp.dot(
+                probs[:, which * keys : (which + 1) * keys],
+                held,
+                preferred_element_type=jnp.float32,
+            )
+            for which in range(m)
+        ]
+        small_part[...] = weight_value * (jnp.where(lanes < lat, terms[0], terms[1]) / totals)
 
     @pl.when(core != 0)
     def _():
         small_part[...] = jnp.zeros_like(small_part)
 
-    for offset in order:
+    for offset in range(1, n):
         for item in (0, 1):
-            big_copy(item, offset, behind(offset)).wait_recv()
+            big_copy(item, behind(offset), offset).wait_recv()
     totals_of = []
     for head in range(heads_here):
         columns = slice(head * DH, (head + 1) * DH)
         probs, totals = softmax_parts(all_q[:, columns], all_k[:, columns])
         weights[head] = probs
         totals_of.append(totals)
-    for offset in order:
-        big_copy(2, offset, behind(offset)).wait_recv()
-    pieces = [
-        weigh(weights[head], totals_of[head], all_v[:, head * DH : (head + 1) * DH])
+    for offset in range(1, n):
+        big_copy(2, behind(offset), offset).wait_recv()
+    held = all_w[...]
+    terms = [
+        jnp.dot(weights[head], held, preferred_element_type=jnp.float32) / totals_of[head]
         for head in range(heads_here)
     ]
-    attended = pieces[0] if heads_here == 1 else jnp.concatenate(pieces, axis=1)
-    term = (1.0 + weight_value) * paired(attended, read_big[...]) - small_part[...]
-    stage[...] = term.reshape(n, half, 2 * lat)
-    arrived[0, core] = stage[me]
-
-    for offset in order + [0]:
+    term = (1.0 + weight_value) * jnp.where(lanes < lat, terms[0], terms[1]) - small_part[...]
+    latent[...] = term + pltpu.roll(term, lat, 1)
+    pair_rows = latent.shape[0] // 2
+    even = latent[pl.ds(0, pair_rows, stride=2), :]
+    odd = latent[pl.ds(1, pair_rows, stride=2), :]
+    paired = jnp.where(lanes[:pair_rows] < lat, even, odd)
+    stage[...] = paired.reshape(n, m, part, 2 * lat)
+    arrived[0, core] = stage[me, core]
+
+    for distance in range(rungs, 0, -1):
+
+        def start_back(peer):
+            for turn in range(m):
+                back_copy(peer, offset_to(peer), turn, core).start()
+
+        toward(distance, start_back)
+    for turn in range(1, m):
+        back_copy(me, 0, turn, core).start()
+    for turn in range(1, m):
+        back_copy(me, 0, turn, lax.rem(core + turn, m)).wait_recv()
+    for offset in range(1, n):
+        for slot_core in range(m):
+            back_copy(behind(offset), offset, 0, slot_core).wait_recv()
+    swap[0] = jnp.sum(arrived[...].reshape(n * m, part, 2 * lat), axis=0)
+    swap_copy().start()
+    out[pl.ds(pl.multiple_of(core * part, part), part), :] = swap[0]
+
+    for offset in range(1, n):
+        for item in (0, 1):
+            few_copy(item, ahead(offset), offset, core).wait_send()
+        for item in range(3):
+            big_copy(item, ahead(offset), offset).wait_send()
         for turn in range(m):
-            if offset or turn:
-                back_copy(offset, turn, core).start()
-    for offset in range(n):
-        for slot_core in range(m):
-            if offset:
-                back_copy(offset, 0, slot_core).wait_recv()
+            back_copy(ahead(offset), offset, turn, core).wait_send()
     for turn in range(1, m):
-        back_copy(0, turn, lax.rem(core + turn, m)).wait_recv()
-    out[...] = jnp.sum(arrived[...].reshape(n * m, half, 2 * lat), axis=0)
-
-    for offset in order:
-        for item in range(3):
-            few_copy(item, offset, me, core).wait_send()
-            big_copy(item, offset, me).wait_send()
+        back_copy(me, 0, turn, core).wait_send()
+
+    @pl.when(core == 0)
+    def _():
+        for offset in range(1, n):
+            few_w_copy(ahead(offset), offset).wait_send()
 
     @pl.when(core != 0)
     def _():
-        for item in range(3):
-            few_copy(item, 0, me, core).wait_send()
-
-    for offset in order + [0]:
-        for turn in range(m):
-            if offset or turn:
-                back_copy(offset, turn, core).wait_send()
+        for item in (0, 1):
+            few_copy(item, me, 0, core).wait_send()
+        core_copy().wait_send()
+
+    swap_copy().wait()
+    out[pl.ds(pl.multiple_of((1 - core) * part, part), part), :] = swap[1]
 
 
 def fused(
@@ -434,35 +565,48 @@
     tokens = rows * n
     lat = big_readout.shape[1]
     half = rows // 2
+    part = half // m
     kind = jnp.bfloat16
     dma = pltpu.SemaphoreType.DMA
     return pl.pallas_call(
-        functools.partial(fused_kernel, n, m),
+        functools.partial(window_kernel, n, m),
         out_shape=pltpu.VMEM((half, 2 * lat), jnp.float32),
         in_specs=[pl.BlockSpec(memory_space=pl.ANY)] * 9,
         out_specs=pl.BlockSpec(memory_space=pltpu.VMEM),
         scratch_shapes=[
             pltpu.VMEM((tokens, width), kind),
             pltpu.VMEM((tokens, width), kind),
-            pltpu.VMEM((tokens, width), kind),
+            pltpu.VMEM((tokens, 2 * lat), kind),
             pltpu.VMEM((tokens, few_width), kind),
             pltpu.VMEM((tokens, few_width), kind),
-            pltpu.VMEM((tokens, few_width), kind),
-            pltpu.VMEM((lat, width), kind),
-            pltpu.VMEM((lat, few_width), kind),
+            pltpu.VMEM((n * few_rows, 2 * lat), kind),
+            pltpu.VMEM((rows, columns), kind),
+            pltpu.VMEM((few_rows, few_columns), kind),
+            pltpu.VMEM((lat, columns), kind),
+            pltpu.VMEM((lat, few_columns), kind),
+            pltpu.VMEM((n, rows, 2 * lat), kind),
+            pltpu.VMEM((n, few_rows, 2 * lat), kind),
+            pltpu.VMEM((n, few_rows, 2 * lat), kind),
+            pltpu.VMEM((n, few_rows, 2 * lat), kind),
             pltpu.VMEM((width // DH, tokens, tokens), kind),
             pltpu.VMEM((tokens, 2 * lat), jnp.float32),
-            pltpu.VMEM((tokens // 2, 2 * lat), jnp.float32),
-            pltpu.VMEM((n, half, 2 * lat), jnp.float32),
-            pltpu.VMEM((n, m, half, 2 * lat), jnp.float32),
+            pltpu.VMEM((tokens, 2 * lat), jnp.float32),
+            pltpu.VMEM((n, m, part, 2 * lat), jnp.float32),
+            pltpu.VMEM((n, m, part, 2 * lat), jnp.float32),
+            pltpu.VMEM((2, part, 2 * lat), jnp.float32),
             pltpu.SMEM((1,), jnp.float32),
+            pltpu.SemaphoreType.REGULAR((n // 2 - 1,)),
             dma((9,)),
             dma((3, n)),
             dma((3, n)),
-            dma((3, n)),
-            dma((3, n, m)),
+            dma((2, n)),
+            dma((2, n, m)),
+            dma((n,)),
+            dma((n,)),
+            dma((2,)),
             dma((n, m)),
             dma((n, m)),
+            dma((2,)),
         ],
         compiler_params=pltpu.CompilerParams(collective_id=0, has_side_effects=True),
         name="fused_window",
@@ -483,11 +627,12 @@
     rows, columns = big_queries.shape
     few_rows, few_columns = small_queries.shape
     return (
-        n > 1
-        and m > 1
+        n > 2
+        and n % 2 == 0
+        and m == 2
         and n * rows <= 512
-        and columns % (n * DH) == 0
-        and few_columns % (n * DH) == 0
+        and columns == 2 * n * DH
+        and few_columns == n * DH
         and rows == m * few_rows
         and few_rows % 16 == 0
         and 2 * lat == 128

time: 27.3 us -> 24.2 us (0.89)
  Pallas kernels: 25.9 us -> 22.8 us
    pallas_call x1, Pallas kernels: 25.9 us -> 22.8 us  [fused(): pl.pallas_call(functools.partial(window_kernel, n, m), out_shape=pltpu.VM...]
where the time goes in v1:
time: 24.2 us; the launch traced here: 24.1 us
  Pallas kernels  22.8 us (94%)
  between operations  0.66 us (3%)
  local copies, waits for them, and re-layouts  0.6 us (2%)
    pallas_call x1, Pallas kernels, fused(): pl.pallas_call(functools.partial(window_kernel, n, m), out_shape=pltpu.VM...  22.8 us
    unnamed x1, local copies, waits for them, and re-layouts  0.6 us

profile of v1, /device:TPU:0, one launch (start us, length us, event | category | flops | bytes accessed | tf_op | source)
XLA Modules:
  0.0 24.1 jit_solution(5900803600960844462)
XLA Ops:
  0.7 22.8 %fused_window.1 = f32[16,128]{1,0:T(8,128)S(1)} custom-call(f32[1]{0:T(128)S(6)} %copy.12.guidance, bf16[32,2048]{1,0:T(8,128)(2,1)} %big_q.1, bf16[32,2048]{1,0:T(8,128)(2,1)} %big_k.1, bf16[32,2048]{1,0:T(8,128)(2,1)} %big_v.1, bf16[16,1024]{1,0:T(8,128)(2,1)} %small_q.1, bf16[16,1024]{1,0:T(8,128)(2,1)} %small_k.1, bf16[16,1024]{1,0:T(8,128)(2,1)} %small_v.1, ...), custom_call_target="tpu_custom_call" | custom-call | tf_op jit(solution)/shard_map/fused_window/pallas_call | solution.py:571
  23.5 0.6 %copy.11 = f32[16,128]{1,0:T(8,128)} copy(f32[16,128]{1,0:T(8,128)S(1)} %fused_window.1) | data formatting | bytes 16384

commit v2 on v1

v2 whole, which is shorter than its diff:
```python
import functools
import math

import jax
import jax.numpy as jnp
from jax import lax
from jax.experimental import pallas as pl
from jax.experimental.pallas import tpu as pltpu
from jax.sharding import PartitionSpec as P

DH = 128


def split_heads(matrix, blocks, parts):
    rows_here, columns = matrix.shape
    shaped = matrix.reshape(blocks, rows_here // blocks, parts, columns // parts)
    shaped = jnp.transpose(shaped, (0, 2, 1, 3))
    return shaped.reshape(blocks * parts, rows_here // blocks, columns // parts)


def copy_heads(matrix, blocks, parts):
    rows_here, columns = matrix.shape
    shaped = jnp.transpose(matrix.reshape(rows_here, parts, columns // parts), (1, 0, 2))
    shaped = jnp.broadcast_to(shaped[None], (blocks, parts, rows_here, columns // parts))
    return shaped.reshape(blocks * parts, rows_here, columns // parts)


def join_heads(stacked, blocks, parts):
    pieces, rows_here, columns = stacked.shape
    shaped = stacked.reshape(blocks, parts, rows_here, columns)
    shaped = jnp.transpose(shaped, (0, 2, 1, 3))
    return shaped.reshape(blocks * rows_here, parts * columns)


def attend(query_rows, key_rows, value_rows):
    query_count = query_rows.shape[0]
    heads_here = query_rows.shape[1] // DH
    key_count = key_rows.shape[0]
    block_height = math.gcd(query_count, 256)
    block_count = query_count // block_height
    query_blocks = query_rows.reshape(block_count, block_height, heads_here, DH)
    key_split = key_rows.reshape(key_count, heads_here, DH)
    value_split = value_rows.reshape(key_count, heads_here, DH)
    score_scale = 1.0 / math.sqrt(DH)

    def one_block(query_block):
        scores = (
            jnp.einsum("qgd,kgd->gqk", query_block, key_split, preferred_element_type=jnp.float32)
            * score_scale
        )
        row_max = jnp.max(scores, axis=2, keepdims=True)
        probs = jnp.exp(scores - row_max)
        totals = jnp.sum(probs, axis=2, keepdims=True)
        weights = probs.astype(jnp.bfloat16)
        accumulated = jnp.einsum(
            "gqk,kgd->gqd", weights, value_split, preferred_element_type=jnp.float32
        )
        attended = accumulated / totals
        attended = jnp.transpose(attended, (1, 0, 2)).reshape(block_height, heads_here * DH)
        return attended.astype(jnp.bfloat16)

    outputs = lax.map(one_block, query_blocks)
    return outputs.reshape(query_count, heads_here * DH)


def exchanged(
    big_queries,
    big_keys,
    big_values,
    small_queries,
    small_keys,
    small_values,
    big_readout,
    small_readout,
    guidance,
):
    seq_count = lax.axis_size("seq")
    big_heads = big_queries.shape[1] // DH
    big_group = max(big_heads // seq_count, 1)
    big_blocks = max(seq_count // big_heads, 1)
    big_parts = big_heads // big_group
    query_rows = lax.all_to_all(
        split_heads(big_queries, big_blocks, big_parts),
        "seq",
        split_axis=0,
        concat_axis=1,
        tiled=True,
    )[0]
    key_copies, value_copies = (
        lax.all_to_all(
            copy_heads(big_keys, big_blocks, big_parts),
            "seq",
            split_axis=0,
            concat_axis=1,
            tiled=True,
        ),
        lax.all_to_all(
            copy_heads(big_values, big_blocks, big_parts),
            "seq",
            split_axis=0,
            concat_axis=1,
            tiled=True,
        ),
    )
    key_rows = key_copies[0]
    value_rows = value_copies[0]
    big_out = attend(query_rows, key_rows, value_rows)
    big_back = lax.all_to_all(big_out[None], "seq", split_axis=1, concat_axis=0, tiled=True)
    big_attention = join_heads(big_back, big_blocks, big_parts)
    big_partial = jnp.dot(big_attention, big_readout, preferred_element_type=jnp.float32)
    small_heads = small_queries.shape[1] // DH
    small_group = max(small_heads // seq_count, 1)
    small_blocks = max(seq_count // small_heads, 1)
    small_parts = small_heads // small_group
    small_query_rows = lax.all_to_all(
        split_heads(small_queries, small_blocks, small_parts),
        "seq",
        split_axis=0,
        concat_axis=1,
        tiled=True,
    )[0]
    key_copies, value_copies = (
        lax.all_to_all(
            copy_heads(small_keys, small_blocks, small_parts),
            "seq",
            split_axis=0,
            concat_axis=1,
            tiled=True,
        ),
        lax.all_to_all(
            copy_heads(small_values, small_blocks, small_parts),
            "seq",
            split_axis=0,
            concat_axis=1,
            tiled=True,
        ),
    )
    small_key_rows, small_value_rows = (
        lax.all_gather(key_copies[0], "head", axis=0, tiled=True),
        lax.all_gather(value_copies[0], "head", axis=0, tiled=True),
    )
    small_out = attend(small_query_rows, small_key_rows, small_value_rows)
    small_back = lax.all_to_all(small_out[None], "seq", split_axis=1, concat_axis=0, tiled=True)
    small_attention = join_heads(small_back, small_blocks, small_parts)
    small_latent = jnp.dot(small_attention, small_readout, preferred_element_type=jnp.float32)
    weight_value = guidance[0]
    core_index = lax.axis_index("head")
    placed = lax.dynamic_update_slice(
        jnp.zeros_like(big_partial),
        small_latent,
        (core_index * small_latent.shape[0], jnp.zeros((), jnp.int32)),
    )
    blended = lax.psum((1.0 + weight_value) * big_partial - weight_value * placed, "head")
    return blended.reshape(blended.shape[0] // 2, 2 * blended.shape[1])


MESH = pl.DeviceIdType.MESH


def softmax_parts(query_head, key_head):
    scores = lax.dot_general(
        query_head, key_head, (((1,), (1,)), ((), ())), preferred_element_type=jnp.float32
    ) * (1.0 / math.sqrt(DH))
    row_max = jnp.max(scores, axis=1, keepdims=True)
    probs = jnp.exp(scores - row_max)
    totals = jnp.sum(probs, axis=1, keepdims=True)
    return probs.astype(jnp.bfloat16), totals


def read_out(values, readout):
    return lax.dot_general(
        values, readout, (((1,), (1,)), ((), ())), preferred_element_type=jnp.float32
    )


def window_kernel(
    n,
    m,
    guidance,
    big_q,
    big_k,
    big_v,
    small_q,
    small_k,
    small_v,
    big_read,
    small_read,
    out,
    all_q,
    all_k,
    all_w,
    few_q,
    few_k,
    few_v,
    own_v,
    read_big,
    read_small,
    ready_w,
    weights,
    small_part,
    latent,
    stage,
    arrived,
    swap,
    guide,
    near,
    own_sem,
    big_send,
    big_recv,
    value_sem,
    few_send,
    few_recv,
    back_sem,
    swap_sem,
):
    group = lax.axis_index("groups")
    me = lax.axis_index("seq")
    core = lax.axis_index("head")
    host = m - 1
    rungs = n // 2
    rung, side = lax.div(me, 2), lax.rem(me, 2)
    rows = big_q.shape[0]
    width = all_q.shape[1]
    few_rows = small_q.shape[0]
    few_width = few_q.shape[1]
    heads_here = width // DH
    lat = big_read.shape[0]
    half = rows // 2
    part = half // m

    def window(ref, index, size):
        return ref.at[:, pl.ds(pl.multiple_of(index * size, size), size)]

    def row_block(ref, index, size):
        return ref.at[pl.ds(pl.multiple_of(index * size, size), size), :]

    def toward(distance, act, crossing=None):
        for up in sorted(range(1 - rungs, rungs), key=lambda up: -abs(up)):
            if distance - abs(up) not in (0, 1):
                continue
            there = rung + up
            wanted = (there >= 0) & (there < rungs)
            if crossing is not None:
                other = (rung < rungs // 2) != (there < rungs // 2)
                wanted = wanted & (other if crossing else jnp.logical_not(other))
            peer = there * 2 + lax.rem(side + distance - abs(up), 2)
            pl.when(wanted)(functools.partial(act, peer))

    def chips_at(distance):
        count = 0
        for up in range(1 - rungs, rungs):
            if distance - abs(up) in (0, 1):
                there = rung + up
                count = count + ((there >= 0) & (there < rungs)).astype(jnp.int32)
        return count

    big_pairs = ((big_k, all_k), (big_q, all_q))
    few_pairs = ((small_k, few_k), (small_q, few_q), (small_v, few_v))

    def head_window(ref, seq, head):
        return ref.at[:, pl.ds(pl.multiple_of(seq * width + head * DH, DH), DH)]

    def head_rows(ref, seq, head):
        return ref.at[pl.ds(pl.multiple_of(seq * rows, rows), rows), pl.ds(head * DH, DH)]

    def big_copy(item, head, peer):
        source, target = big_pairs[item]
        return pltpu.make_async_remote_copy(
            src_ref=head_window(source, peer, head),
            dst_ref=head_rows(target, me, head),
            send_sem=big_send.at[item],
            recv_sem=big_recv.at[item, head],
            device_id=(group, peer, core),
            device_id_type=MESH,
        )

    def value_copy(peer):
        return pltpu.make_async_remote_copy(
            src_ref=ready_w.at[peer],
            dst_ref=row_block(all_w, me, rows),
            send_sem=value_sem.at[0],
            recv_sem=value_sem.at[1],
            device_id=(group, peer, core),
            device_id_type=MESH,
        )

    def few_copy(item, peer):
        source, target = few_pairs[item]
        return pltpu.make_async_remote_copy(
            src_ref=window(source, peer, few_width),
            dst_ref=row_block(target, me * m + core, few_rows),
            send_sem=few_send.at[item],
            recv_sem=few_recv.at[item],
            device_id=(group, peer, host),
            device_id_type=MESH,
        )

    def back_copy(peer, which):
        return pltpu.make_async_remote_copy(
            src_ref=stage.at[peer * m + which],
            dst_ref=arrived.at[me * m + core],
            send_sem=back_sem.at[0],
            recv_sem=back_sem.at[1],
            device_id=(group, peer, which),
            device_id_type=MESH,
        )

    def swap_copy():
        return pltpu.make_async_remote_copy(
            src_ref=swap.at[0],
            dst_ref=swap.at[1],
            send_sem=swap_sem.at[0],
            recv_sem=swap_sem.at[1],
            device_id=(group, me, 1 - core),
            device_id_type=MESH,
        )

    def await_bytes(ref, sem):
        pltpu.make_async_copy(ref, ref, sem).wait()

    barrier = pltpu.get_barrier_semaphore()

    def greet(peer):
        for which in range(m):
            pl.semaphore_signal(
                barrier, inc=1, device_id=(group, peer, which), device_id_type=MESH
            )

    toward(1, greet)
    pl.semaphore_signal(
        barrier, inc=1, device_id=(group, me, 1 - core), device_id_type=MESH
    )

    value_copies = [
        pltpu.make_async_copy(big_v, own_v, own_sem.at[0]),
        pltpu.make_async_copy(big_read, read_big, own_sem.at[1]),
    ]
    for copy in value_copies:
        copy.start()
    late_copies = [
        pltpu.make_async_copy(guidance, guide, own_sem.at[2]),
        pltpu.make_async_copy(window(small_read, me, few_width), read_small, own_sem.at[3]),
    ]
    for copy in late_copies:
        copy.start()
    for head in range(heads_here):
        for item, (source, target) in enumerate(big_pairs):
            pltpu.make_async_copy(
                head_window(source, me, head),
                head_rows(target, me, head),
                big_recv.at[item, head],
            ).start()

    @pl.when(core == host)
    def _():
        for item in range(3):
            source, target = few_pairs[item]
            pltpu.make_async_copy(
                window(source, me, few_width),
                row_block(target, me * m + host, few_rows),
                few_recv.at[item],
            ).start()

    for copy in value_copies:
        copy.wait()
    for seq in range(n):
        terms = []
        for head in range(heads_here):
            columns = slice(seq * width + head * DH, seq * width + (head + 1) * DH)
            terms.append(read_out(own_v[:, columns], read_big[:, columns]))
        ready_w[seq] = jnp.concatenate(terms, axis=1).astype(ready_w.dtype)

    def start_few(peer):
        for item in range(3):
            few_copy(item, peer).start()

    def start_head(head, peer):
        for item in (0, 1):
            big_copy(item, head, peer).start()

    def start_early(peer):
        start_few(peer)
        start_head(0, peer)
        value_copy(peer).start()

    def start_late(peer):
        for head in range(1, heads_here):
            start_head(head, peer)

    def pass_on(index):
        def act(peer):
            pl.semaphore_signal(
                near.at[index], inc=1, device_id=(group, peer, core), device_id_type=MESH
            )

        return act

    pl.semaphore_wait(barrier, m * chips_at(1) + m - 1)
    toward(1, pass_on(0))
    toward(1, start_early, True)
    toward(1, start_late, True)
    toward(1, start_early, False)
    known, index = 1, 0
    while known < rungs:
        pl.semaphore_wait(near.at[index], chips_at(known))
        reach = min(2 * known, rungs)
        index += 1
        if reach < rungs:
            toward(reach, pass_on(index))
        for distance in range(known + 1, reach + 1):
            toward(distance, start_early, True)
            toward(distance, start_early, False)
        held, known = known, reach
    for distance in range(held + 1, rungs + 1):
        toward(distance, start_late)
    for distance in range(held, 1, -1):
        toward(distance, start_late)
    toward(1, start_late, False)

    @pl.when(core != host)
    def _():
        for item in range(3):
            few_copy(item, me).start()

    all_w[pl.ds(pl.multiple_of(me * rows, rows), rows), :] = ready_w[me]
    for copy in late_copies:
        copy.wait()
    weight_value = guide[0]
    lanes = lax.broadcasted_iota(jnp.int32, latent.shape, 1)

    @pl.when(core == host)
    def _():
        for item in range(3):
            await_bytes(few_pairs[item][1], few_recv.at[item])
        probs, totals = softmax_parts(few_q[...], few_k[...])
        attended = jnp.dot(probs, few_v[...], preferred_element_type=jnp.float32) / totals
        term = read_out(attended.astype(few_v.dtype), read_small[...])
        small_part[...] = weight_value * jnp.concatenate([term, jnp.zeros_like(term)], axis=1)

    @pl.when(core != host)
    def _():
        small_part[...] = jnp.zeros_like(small_part)

    for head in range(heads_here):
        columns = slice(head * DH, (head + 1) * DH)
        for item, (source, target) in enumerate(big_pairs):
            await_bytes(target.at[:, columns], big_recv.at[item, head])
        probs, totals = softmax_parts(all_q[:, columns], all_k[:, columns])
        if head == 0:
            weights[...] = probs
            await_bytes(all_w.at[pl.ds(0, (n - 1) * rows), :], value_sem.at[1])
            probs = weights[...]
        term = jnp.dot(probs, all_w[...], preferred_element_type=jnp.float32) / totals
        term = (1.0 + weight_value) * term
        if head == 0:
            small_part[...] = term - small_part[...]
    term = jnp.where(lanes < lat, small_part[...], term)
    latent[...] = term + pltpu.roll(term, lat, 1)
    pair_rows = latent.shape[0] // 2
    even = latent[pl.ds(0, pair_rows, stride=2), :]
    odd = latent[pl.ds(1, pair_rows, stride=2), :]
    paired = jnp.where(lanes[:pair_rows] < lat, even, odd)
    stage[...] = paired.reshape(n * m, part, 2 * lat)
    arrived[me * m + core] = stage[me * m + core]

    def start_back(peer):
        for which in range(m):
            back_copy(peer, which).start()

    for distance in range(rungs, 0, -1):
        toward(distance, start_back)
    back_copy(me, 1 - core).start()
    everyone = arrived.at[pl.ds(0, n * m - 1)]
    await_bytes(everyone, back_sem.at[1])
    swap[0] = jnp.sum(arrived[...], axis=0)
    swap_copy().start()
    out[pl.ds(pl.multiple_of(core * part, part), part), :] = swap[0]

    for item in (0, 1):
        await_bytes(big_pairs[item][1].at[pl.ds(0, (n - 1) * rows), :], big_send.at[item])
    await_bytes(all_w.at[pl.ds(0, (n - 1) * rows), :], value_sem.at[0])
    await_bytes(everyone, back_sem.at[0])

    @pl.when(core == host)
    def _():
        for item in range(3):
            await_bytes(few_pairs[item][1].at[pl.ds(0, (n - 1) * few_rows), :], few_send.at[item])

    @pl.when(core != host)
    def _():
        for item in range(3):
            await_bytes(few_pairs[item][1].at[pl.ds(0, n * few_rows), :], few_send.at[item])

    swap_copy().wait()
    out[pl.ds(pl.multiple_of((1 - core) * part, part), part), :] = swap[1]


def fused(
    n,
    m,
    big_queries,
    big_keys,
    big_values,
    small_queries,
    small_keys,
    small_values,
    big_readout,
    small_readout,
    guidance,
):
    rows, columns = big_queries.shape
    few_rows, few_columns = small_queries.shape
    width, few_width = columns // n, few_columns // n
    tokens = rows * n
    lat = big_readout.shape[1]
    half = rows // 2
    part = half // m
    kind = jnp.bfloat16
    dma = pltpu.SemaphoreType.DMA
    return pl.pallas_call(
        functools.partial(window_kernel, n, m),
        out_shape=pltpu.VMEM((half, 2 * lat), jnp.float32),
        in_specs=[pl.BlockSpec(memory_space=pl.ANY)] * 9,
        out_specs=pl.BlockSpec(memory_space=pltpu.VMEM),
        scratch_shapes=[
            pltpu.VMEM((tokens, width), kind),
            pltpu.VMEM((tokens, width), kind),
            pltpu.VMEM((tokens, 2 * lat), kind),
            pltpu.VMEM((tokens, few_width), kind),
            pltpu.VMEM((tokens, few_width), kind),
            pltpu.VMEM((tokens, few_width), kind),
            pltpu.VMEM((rows, columns), kind),
            pltpu.VMEM((lat, columns), kind),
            pltpu.VMEM((lat, few_width), kind),
            pltpu.VMEM((n, rows, 2 * lat), kind),
            pltpu.VMEM((tokens, tokens), kind),
            pltpu.VMEM((tokens, 2 * lat), jnp.float32),
            pltpu.VMEM((tokens, 2 * lat), jnp.float32),
            pltpu.VMEM((n * m, part, 2 * lat), jnp.float32),
            pltpu.VMEM((n * m, part, 2 * lat), jnp.float32),
            pltpu.VMEM((2, part, 2 * lat), jnp.float32),
            pltpu.SMEM((1,), jnp.float32),
            pltpu.SemaphoreType.REGULAR(((n // 2 - 1).bit_length(),)),
            dma((4,)),
            dma((2,)),
            dma((2, width // DH)),
            dma((2,)),
            dma((3,)),
            dma((3,)),
            dma((2,)),
            dma((2,)),
        ],
        compiler_params=pltpu.CompilerParams(collective_id=0, has_side_effects=True),
        name="fused_window",
    )(
        guidance,
        big_queries,
        big_keys,
        big_values,
        small_queries,
        small_keys,
        small_values,
        big_readout.T,
        small_readout.T,
    )


def fits(n, m, big_queries, small_queries, lat):
    rows, columns = big_queries.shape
    few_rows, few_columns = small_queries.shape
    return (
        n > 2
        and n % 2 == 0
        and m == 2
        and n * rows <= 512
        and columns == 2 * n * DH
        and few_columns == n * DH
        and rows == m * few_rows
        and few_rows % 16 == 0
        and 2 * lat == 128
    )


def shards(*arguments):
    n, m = lax.axis_size("seq"), lax.axis_size("head")
    if fits(n, m, arguments[0], arguments[3], arguments[6].shape[1]):
        return fused(n, m, *arguments)
    return exchanged(*arguments)


def solution(mesh):
    placed = (
        P(("groups", "seq"), "head"),
        P(("groups", "seq"), "head"),
        P(("groups", "seq"), "head"),
        P(("groups", "seq", "head"), None),
        P(("groups", "seq", "head"), None),
        P(("groups", "seq", "head"), None),
        P("head", None),
        P(),
        P("groups"),
    )
    return jax.shard_map(
        shards, mesh=mesh, in_specs=placed, out_specs=P(("groups", "seq"), None), check_vma=False
    )
```

time: 24.2 us -> 22.8 us (0.942)
  Pallas kernels: 22.8 us -> 21.4 us
    pallas_call x1, Pallas kernels: 22.8 us -> 21.4 us  [fused(): pl.pallas_call(functools.partial(window_kernel, n, m), out_shape=pltpu.VM...]
where the time goes in v2:
time: 22.8 us; the launch traced here: 22.6 us
  Pallas kernels  21.4 us (94%)
  between operations  0.66 us (3%)
  local copies, waits for them, and re-layouts  0.6 us (3%)
    pallas_call x1, Pallas kernels, fused(): pl.pallas_call(functools.partial(window_kernel, n, m), out_shape=pltpu.VM...  21.4 us
    unnamed x1, local copies, waits for them, and re-layouts  0.6 us

profile of v2, /device:TPU:0, one launch (start us, length us, event | category | flops | bytes accessed | tf_op | source)
XLA Modules:
  0.0 22.6 jit_solution(11603384041385758033)
XLA Ops:
  0.7 21.4 %fused_window.1 = f32[16,128]{1,0:T(8,128)S(1)} custom-call(f32[1]{0:T(128)S(6)} %copy.12.guidance, bf16[32,2048]{1,0:T(8,128)(2,1)} %big_q.1, bf16[32,2048]{1,0:T(8,128)(2,1)} %big_k.1, bf16[32,2048]{1,0:T(8,128)(2,1)} %big_v.1, bf16[16,1024]{1,0:T(8,128)(2,1)} %small_q.1, bf16[16,1024]{1,0:T(8,128)(2,1)} %small_k.1, bf16[16,1024]{1,0:T(8,128)(2,1)} %small_v.1, ...), custom_call_target="tpu_custom_call" | custom-call | tf_op jit(solution)/shard_map/fused_window/pallas_call | solution.py:520
  22.0 0.6 %copy.11 = f32[16,128]{1,0:T(8,128)} copy(f32[16,128]{1,0:T(8,128)S(1)} %fused_window.1) | data formatting | bytes 16384

commit v3 on v2

--- a/solution.py
+++ b/solution.py
@@ -196,9 +196,9 @@
     read_big,
     read_small,
     ready_w,
-    weights,
     small_part,
     latent,
+    first_stage,
     stage,
     arrived,
     swap,
@@ -220,6 +220,7 @@
     rungs = n // 2
     rung, side = lax.div(me, 2), lax.rem(me, 2)
     rows = big_q.shape[0]
+    tokens = n * rows
     width = all_q.shape[1]
     few_rows = small_q.shape[0]
     few_width = few_q.shape[1]
@@ -254,22 +255,25 @@
                 count = count + ((there >= 0) & (there < rungs)).astype(jnp.int32)
         return count
 
-    big_pairs = ((big_k, all_k), (big_q, all_q))
-    few_pairs = ((small_k, few_k), (small_q, few_q), (small_v, few_v))
-
-    def head_window(ref, seq, head):
-        return ref.at[:, pl.ds(pl.multiple_of(seq * width + head * DH, DH), DH)]
-
-    def head_rows(ref, seq, head):
-        return ref.at[pl.ds(pl.multiple_of(seq * rows, rows), rows), pl.ds(head * DH, DH)]
-
-    def big_copy(item, head, peer):
-        source, target = big_pairs[item]
+    behind = (me != 0).astype(jnp.int32)
+    few_pairs = ((small_k, few_k), (small_v, few_v), (small_q, few_q))
+
+    def key_copy(peer):
         return pltpu.make_async_remote_copy(
-            src_ref=head_window(source, peer, head),
-            dst_ref=head_rows(target, me, head),
-            send_sem=big_send.at[item],
-            recv_sem=big_recv.at[item, head],
+            src_ref=window(big_k, peer, width),
+            dst_ref=row_block(all_k, me, rows),
+            send_sem=big_send.at[0],
+            recv_sem=big_recv.at[0],
+            device_id=(group, peer, core),
+            device_id_type=MESH,
+        )
+
+    def query_copy(peer):
+        return pltpu.make_async_remote_copy(
+            src_ref=window(big_q, peer, width),
+            dst_ref=row_block(all_q, me, rows),
+            send_sem=big_send.at[1],
+            recv_sem=big_recv.at[1 + behind],
             device_id=(group, peer, core),
             device_id_type=MESH,
         )
@@ -290,14 +294,14 @@
             src_ref=window(source, peer, few_width),
             dst_ref=row_block(target, me * m + core, few_rows),
             send_sem=few_send.at[item],
-            recv_sem=few_recv.at[item],
+            recv_sem=few_recv.at[item + behind if item == 2 else item],
             device_id=(group, peer, host),
             device_id_type=MESH,
         )
 
-    def back_copy(peer, which):
+    def back_copy(peer, which, source):
         return pltpu.make_async_remote_copy(
-            src_ref=stage.at[peer * m + which],
+            src_ref=source,
             dst_ref=arrived.at[me * m + core],
             send_sem=back_sem.at[0],
             recv_sem=back_sem.at[1],
@@ -343,22 +347,21 @@
     ]
     for copy in late_copies:
         copy.start()
-    for head in range(heads_here):
-        for item, (source, target) in enumerate(big_pairs):
-            pltpu.make_async_copy(
-                head_window(source, me, head),
-                head_rows(target, me, head),
-                big_recv.at[item, head],
-            ).start()
+    pltpu.make_async_copy(
+        window(big_k, me, width), row_block(all_k, me, rows), big_recv.at[0]
+    ).start()
+
+    pltpu.make_async_copy(
+        window(big_q, me, width), row_block(all_q, me, rows), big_recv.at[1 + behind]
+    ).start()
 
     @pl.when(core == host)
     def _():
-        for item in range(3):
-            source, target = few_pairs[item]
+        for item, (source, target) in enumerate(few_pairs):
             pltpu.make_async_copy(
                 window(source, me, few_width),
                 row_block(target, me * m + host, few_rows),
-                few_recv.at[item],
+                few_recv.at[item + behind if item == 2 else item],
             ).start()
 
     for copy in value_copies:
@@ -370,22 +373,19 @@
             terms.append(read_out(own_v[:, columns], read_big[:, columns]))
         ready_w[seq] = jnp.concatenate(terms, axis=1).astype(ready_w.dtype)
 
-    def start_few(peer):
-        for item in range(3):
+    def start_queries(peer):
+        few_copy(2, peer).start()
+        query_copy(peer).start()
+
+    def start_early(peer):
+        for item in (0, 1):
             few_copy(item, peer).start()
-
-    def start_head(head, peer):
-        for item in (0, 1):
-            big_copy(item, head, peer).start()
-
-    def start_early(peer):
-        start_few(peer)
-        start_head(0, peer)
+        key_copy(peer).start()
         value_copy(peer).start()
+        pl.when(me == 0)(functools.partial(start_queries, peer))
 
     def start_late(peer):
-        for head in range(1, heads_here):
-            start_head(head, peer)
+        pl.when(me != 0)(functools.partial(start_queries, peer))
 
     def pass_on(index):
         def act(peer):
@@ -426,59 +426,109 @@
     for copy in late_copies:
         copy.wait()
     weight_value = guide[0]
-    lanes = lax.broadcasted_iota(jnp.int32, latent.shape, 1)
+
+    def attend_rows(first, count, few_waits, head_waits):
+        block = pl.ds(first, count)
+        lanes = lax.broadcasted_iota(jnp.int32, (count, 2 * lat), 1)
+
+        @pl.when(core == host)
+        def _():
+            few_waits()
+            probs, totals = softmax_parts(few_q[block, :], few_k[...])
+            attended = jnp.dot(probs, few_v[...], preferred_element_type=jnp.float32) / totals
+            term = read_out(attended.astype(few_v.dtype), read_small[...])
+            small_part[block, :] = weight_value * jnp.concatenate(
+                [term, jnp.zeros_like(term)], axis=1
+            )
+
+        @pl.when(core != host)
+        def _():
+            small_part[block, :] = jnp.zeros((count, 2 * lat), jnp.float32)
+
+        for head in range(heads_here):
+            head_waits(head)
+            columns = slice(head * DH, (head + 1) * DH)
+            probs, totals = softmax_parts(all_q[block, columns], all_k[:, columns])
+            term = jnp.dot(probs, all_w[...], preferred_element_type=jnp.float32) / totals
+            term = (1.0 + weight_value) * term
+            if head == 0:
+                small_part[block, :] = term - small_part[block, :]
+        term = jnp.where(lanes < lat, small_part[block, :], term)
+        latent[block, :] = term + pltpu.roll(term, lat, 1)
+        pair_rows = count // 2
+        even = latent[pl.ds(first, pair_rows, stride=2), :]
+        odd = latent[pl.ds(first + 1, pair_rows, stride=2), :]
+        return jnp.where(lanes[:pair_rows] < lat, even, odd)
+
+    later = tokens - rows
+
+    def first_few_waits():
+        await_bytes(few_q.at[pl.ds(0, rows), :], few_recv.at[2])
+
+    def later_few_waits():
+        await_bytes(few_q.at[pl.ds(0, later), :], few_recv.at[3])
+
+    def first_head_waits(head):
+        if head == 0:
+            await_bytes(all_q.at[pl.ds(0, rows), :], big_recv.at[1])
+
+    def later_head_waits(head):
+        if head == 0:
+            await_bytes(all_q.at[pl.ds(0, later), :], big_recv.at[2])
+
+    def attend_first():
+        first_stage[...] = attend_rows(0, rows, first_few_waits, first_head_waits).reshape(
+            m, part, 2 * lat
+        )
 
     @pl.when(core == host)
     def _():
-        for item in range(3):
+        for item in (0, 1):
             await_bytes(few_pairs[item][1], few_recv.at[item])
-        probs, totals = softmax_parts(few_q[...], few_k[...])
-        attended = jnp.dot(probs, few_v[...], preferred_element_type=jnp.float32) / totals
-        term = read_out(attended.astype(few_v.dtype), read_small[...])
-        small_part[...] = weight_value * jnp.concatenate([term, jnp.zeros_like(term)], axis=1)
-
-    @pl.when(core != host)
-    def _():
-        small_part[...] = jnp.zeros_like(small_part)
-
-    for head in range(heads_here):
-        columns = slice(head * DH, (head + 1) * DH)
-        for item, (source, target) in enumerate(big_pairs):
-            await_bytes(target.at[:, columns], big_recv.at[item, head])
-        probs, totals = softmax_parts(all_q[:, columns], all_k[:, columns])
-        if head == 0:
-            weights[...] = probs
-            await_bytes(all_w.at[pl.ds(0, (n - 1) * rows), :], value_sem.at[1])
-            probs = weights[...]
-        term = jnp.dot(probs, all_w[...], preferred_element_type=jnp.float32) / totals
-        term = (1.0 + weight_value) * term
-        if head == 0:
-            small_part[...] = term - small_part[...]
-    term = jnp.where(lanes < lat, small_part[...], term)
-    latent[...] = term + pltpu.roll(term, lat, 1)
-    pair_rows = latent.shape[0] // 2
-    even = latent[pl.ds(0, pair_rows, stride=2), :]
-    odd = latent[pl.ds(1, pair_rows, stride=2), :]
-    paired = jnp.where(lanes[:pair_rows] < lat, even, odd)
-    stage[...] = paired.reshape(n * m, part, 2 * lat)
-    arrived[me * m + core] = stage[me * m + core]
+
+    await_bytes(all_k, big_recv.at[0])
+    await_bytes(all_w.at[pl.ds(0, later), :], value_sem.at[1])
+
+    @pl.when(me != 0)
+    def _():
+        attend_first()
+        for which in range(m):
+            back_copy(0, which, first_stage.at[which]).start()
+
+    stage[...] = attend_rows(rows, later, later_few_waits, later_head_waits).reshape(
+        (n - 1) * m, part, 2 * lat
+    )
 
     def start_back(peer):
-        for which in range(m):
-            back_copy(peer, which).start()
+        @pl.when(peer != 0)
+        def _():
+            for which in range(m):
+                back_copy(peer, which, stage.at[(peer - 1) * m + which]).start()
 
     for distance in range(rungs, 0, -1):
         toward(distance, start_back)
-    back_copy(me, 1 - core).start()
+
+    @pl.when(me != 0)
+    def _():
+        own = (me - 1) * m
+        arrived[me * m + core] = stage[own + core]
+        back_copy(me, 1 - core, stage.at[own + 1 - core]).start()
+
+    @pl.when(me == 0)
+    def _():
+        attend_first()
+        arrived[core] = first_stage[core]
+        back_copy(0, 1 - core, first_stage.at[1 - core]).start()
+
     everyone = arrived.at[pl.ds(0, n * m - 1)]
     await_bytes(everyone, back_sem.at[1])
     swap[0] = jnp.sum(arrived[...], axis=0)
     swap_copy().start()
     out[pl.ds(pl.multiple_of(core * part, part), part), :] = swap[0]
 
-    for item in (0, 1):
-        await_bytes(big_pairs[item][1].at[pl.ds(0, (n - 1) * rows), :], big_send.at[item])
-    await_bytes(all_w.at[pl.ds(0, (n - 1) * rows), :], value_sem.at[0])
+    await_bytes(all_k.at[pl.ds(0, later), :], big_send.at[0])
+    await_bytes(all_q.at[pl.ds(0, later), :], big_send.at[1])
+    await_bytes(all_w.at[pl.ds(0, later), :], value_sem.at[0])
     await_bytes(everyone, back_sem.at[0])
 
     @pl.when(core == host)
@@ -533,20 +583,20 @@
             pltpu.VMEM((lat, columns), kind),
             pltpu.VMEM((lat, few_width), kind),
             pltpu.VMEM((n, rows, 2 * lat), kind),
-            pltpu.VMEM((tokens, tokens), kind),
             pltpu.VMEM((tokens, 2 * lat), jnp.float32),
             pltpu.VMEM((tokens, 2 * lat), jnp.float32),
-            pltpu.VMEM((n * m, part, 2 * lat), jnp.float32),
+            pltpu.VMEM((m, part, 2 * lat), jnp.float32),
+            pltpu.VMEM(((n - 1) * m, part, 2 * lat), jnp.float32),
             pltpu.VMEM((n * m, part, 2 * lat), jnp.float32),
             pltpu.VMEM((2, part, 2 * lat), jnp.float32),
             pltpu.SMEM((1,), jnp.float32),
             pltpu.SemaphoreType.REGULAR(((n // 2 - 1).bit_length(),)),
             dma((4,)),
             dma((2,)),
-            dma((2, width // DH)),
+            dma((3,)),
             dma((2,)),
             dma((3,)),
-            dma((3,)),
+            dma((4,)),
             dma((2,)),
             dma((2,)),
         ],

time: 22.8 us -> 22.4 us (0.982)
  Pallas kernels: 21.4 us -> 21 us
    pallas_call x1, Pallas kernels: 21.4 us -> 21 us  [fused(): pl.pallas_call(functools.partial(window_kernel, n, m), out_shape=pltpu.VM...]
where the time goes in v3:
time: 22.4 us; the launch traced here: 22.3 us
  Pallas kernels  21 us (94%)
  between operations  0.66 us (3%)
  local copies, waits for them, and re-layouts  0.6 us (3%)
    pallas_call x1, Pallas kernels, fused(): pl.pallas_call(functools.partial(window_kernel, n, m), out_shape=pltpu.VM...  21 us
    unnamed x1, local copies, waits for them, and re-layouts  0.6 us

profile of v3, /device:TPU:0, one launch (start us, length us, event | category | flops | bytes accessed | tf_op | source)
XLA Modules:
  0.0 22.3 jit_solution(3236170747127256939)
XLA Ops:
  0.7 21.0 %fused_window.1 = f32[16,128]{1,0:T(8,128)S(1)} custom-call(f32[1]{0:T(128)S(6)} %copy.12.guidance, bf16[32,2048]{1,0:T(8,128)(2,1)} %big_q.1, bf16[32,2048]{1,0:T(8,128)(2,1)} %big_k.1, bf16[32,2048]{1,0:T(8,128)(2,1)} %big_v.1, bf16[16,1024]{1,0:T(8,128)(2,1)} %small_q.1, bf16[16,1024]{1,0:T(8,128)(2,1)} %small_k.1, bf16[16,1024]{1,0:T(8,128)(2,1)} %small_v.1, ...), custom_call_target="tpu_custom_call" | custom-call | tf_op jit(solution)/shard_map/fused_window/pallas_call | solution.py:570
  21.7 0.6 %copy.11 = f32[16,128]{1,0:T(8,128)} copy(f32[16,128]{1,0:T(8,128)S(1)} %fused_window.1) | data formatting | bytes 16384

commit v4 on v3

--- a/solution.py
+++ b/solution.py
@@ -191,11 +191,13 @@
     all_w,
     few_q,
     few_k,
-    few_v,
+    few_w,
     own_v,
+    own_few_v,
     read_big,
     read_small,
     ready_w,
+    ready_few,
     small_part,
     latent,
     first_stage,
@@ -256,7 +258,7 @@
         return count
 
     behind = (me != 0).astype(jnp.int32)
-    few_pairs = ((small_k, few_k), (small_v, few_v), (small_q, few_q))
+    few_pairs = ((small_k, few_k), (ready_few, few_w), (small_q, few_q))
 
     def key_copy(peer):
         return pltpu.make_async_remote_copy(
@@ -291,8 +293,12 @@
     def few_copy(item, peer):
         source, target = few_pairs[item]
         return pltpu.make_async_remote_copy(
-            src_ref=window(source, peer, few_width),
-            dst_ref=row_block(target, me * m + core, few_rows),
+            src_ref=source.at[peer] if item == 1 else window(source, peer, few_width),
+            dst_ref=(
+                target.at[me * m + core]
+                if item == 1
+                else row_block(target, me * m + core, few_rows)
+            ),
             send_sem=few_send.at[item],
             recv_sem=few_recv.at[item + behind if item == 2 else item],
             device_id=(group, peer, host),
@@ -338,15 +344,13 @@
     value_copies = [
         pltpu.make_async_copy(big_v, own_v, own_sem.at[0]),
         pltpu.make_async_copy(big_read, read_big, own_sem.at[1]),
+        pltpu.make_async_copy(small_v, own_few_v, own_sem.at[2]),
+        pltpu.make_async_copy(small_read, read_small, own_sem.at[3]),
     ]
     for copy in value_copies:
         copy.start()
-    late_copies = [
-        pltpu.make_async_copy(guidance, guide, own_sem.at[2]),
-        pltpu.make_async_copy(window(small_read, me, few_width), read_small, own_sem.at[3]),
-    ]
-    for copy in late_copies:
-        copy.start()
+    guide_copy = pltpu.make_async_copy(guidance, guide, own_sem.at[4])
+    guide_copy.start()
     pltpu.make_async_copy(
         window(big_k, me, width), row_block(all_k, me, rows), big_recv.at[0]
     ).start()
@@ -357,7 +361,8 @@
 
     @pl.when(core == host)
     def _():
-        for item, (source, target) in enumerate(few_pairs):
+        for item in (0, 2):
+            source, target = few_pairs[item]
             pltpu.make_async_copy(
                 window(source, me, few_width),
                 row_block(target, me * m + host, few_rows),
@@ -372,6 +377,10 @@
             columns = slice(seq * width + head * DH, seq * width + (head + 1) * DH)
             terms.append(read_out(own_v[:, columns], read_big[:, columns]))
         ready_w[seq] = jnp.concatenate(terms, axis=1).astype(ready_w.dtype)
+        columns = slice(seq * few_width, (seq + 1) * few_width)
+        term = read_out(own_few_v[:, columns], read_small[:, columns])
+        term = jnp.concatenate([term[: few_rows // 2], term[few_rows // 2 :]], axis=1)
+        ready_few[seq] = term.astype(ready_few.dtype)
 
     def start_queries(peer):
         few_copy(2, peer).start()
@@ -398,7 +407,6 @@
     pl.semaphore_wait(barrier, m * chips_at(1) + m - 1)
     toward(1, pass_on(0))
     toward(1, start_early, True)
-    toward(1, start_late, True)
     toward(1, start_early, False)
     known, index = 1, 0
     while known < rungs:
@@ -413,9 +421,8 @@
         held, known = known, reach
     for distance in range(held + 1, rungs + 1):
         toward(distance, start_late)
-    for distance in range(held, 1, -1):
+    for distance in range(held, 0, -1):
         toward(distance, start_late)
-    toward(1, start_late, False)
 
     @pl.when(core != host)
     def _():
@@ -423,8 +430,7 @@
             few_copy(item, me).start()
 
     all_w[pl.ds(pl.multiple_of(me * rows, rows), rows), :] = ready_w[me]
-    for copy in late_copies:
-        copy.wait()
+    guide_copy.wait()
     weight_value = guide[0]
 
     def attend_rows(first, count, few_waits, head_waits):
@@ -435,11 +441,14 @@
         def _():
             few_waits()
             probs, totals = softmax_parts(few_q[block, :], few_k[...])
-            attended = jnp.dot(probs, few_v[...], preferred_element_type=jnp.float32) / totals
-            term = read_out(attended.astype(few_v.dtype), read_small[...])
-            small_part[block, :] = weight_value * jnp.concatenate(
-                [term, jnp.zeros_like(term)], axis=1
-            )
+            pairs = few_w[...].astype(jnp.float32).reshape(n * m * few_rows // 2, 2 * lat)
+            sides = [
+                side.reshape(n * m, few_rows // 2, 2 * lat)
+                for side in (pairs, pltpu.roll(pairs, lat, 1))
+            ]
+            held = jnp.concatenate(sides, axis=1).reshape(tokens, 2 * lat)
+            term = jnp.dot(probs, held.astype(few_w.dtype), preferred_element_type=jnp.float32)
+            small_part[block, :] = weight_value * term / totals
 
         @pl.when(core != host)
         def _():
@@ -483,8 +492,9 @@
 
     @pl.when(core == host)
     def _():
-        for item in (0, 1):
-            await_bytes(few_pairs[item][1], few_recv.at[item])
+        few_w[me * m + host] = ready_few[me]
+        await_bytes(few_k, few_recv.at[0])
+        await_bytes(few_w.at[pl.ds(0, n * m - 1)], few_recv.at[1])
 
     await_bytes(all_k, big_recv.at[0])
     await_bytes(all_w.at[pl.ds(0, later), :], value_sem.at[1])
@@ -531,15 +541,13 @@
     await_bytes(all_w.at[pl.ds(0, later), :], value_sem.at[0])
     await_bytes(everyone, back_sem.at[0])
 
-    @pl.when(core == host)
-    def _():
-        for item in range(3):
-            await_bytes(few_pairs[item][1].at[pl.ds(0, (n - 1) * few_rows), :], few_send.at[item])
-
-    @pl.when(core != host)
-    def _():
-        for item in range(3):
-            await_bytes(few_pairs[item][1].at[pl.ds(0, n * few_rows), :], few_send.at[item])
+    def await_few(chips):
+        for item in (0, 2):
+            await_bytes(few_pairs[item][1].at[pl.ds(0, chips * few_rows), :], few_send.at[item])
+        await_bytes(few_w.at[pl.ds(0, chips)], few_send.at[1])
+
+    pl.when(core == host)(functools.partial(await_few, n - 1))
+    pl.when(core != host)(functools.partial(await_few, n))
 
     swap_copy().wait()
     out[pl.ds(pl.multiple_of((1 - core) * part, part), part), :] = swap[1]
@@ -578,11 +586,13 @@
             pltpu.VMEM((tokens, 2 * lat), kind),
             pltpu.VMEM((tokens, few_width), kind),
             pltpu.VMEM((tokens, few_width), kind),
-            pltpu.VMEM((tokens, few_width), kind),
+            pltpu.VMEM((n * m, few_rows // 2, 2 * lat), kind),
             pltpu.VMEM((rows, columns), kind),
+            pltpu.VMEM((few_rows, few_columns), kind),
             pltpu.VMEM((lat, columns), kind),
-            pltpu.VMEM((lat, few_width), kind),
+            pltpu.VMEM((lat, few_columns), kind),
             pltpu.VMEM((n, rows, 2 * lat), kind),
+            pltpu.VMEM((n, few_rows // 2, 2 * lat), kind),
             pltpu.VMEM((tokens, 2 * lat), jnp.float32),
             pltpu.VMEM((tokens, 2 * lat), jnp.float32),
             pltpu.VMEM((m, part, 2 * lat), jnp.float32),
@@ -591,7 +601,7 @@
             pltpu.VMEM((2, part, 2 * lat), jnp.float32),
             pltpu.SMEM((1,), jnp.float32),
             pltpu.SemaphoreType.REGULAR(((n // 2 - 1).bit_length(),)),
-            dma((4,)),
+            dma((5,)),
             dma((2,)),
             dma((3,)),
             dma((2,)),

time: 22.4 us -> 22 us (0.982)
  Pallas kernels: 21 us -> 20.6 us
    pallas_call x1, Pallas kernels: 21 us -> 20.6 us  [fused(): pl.pallas_call(functools.partial(window_kernel, n, m), out_shape=pltpu.VM...]
where the time goes in v4:
time: 22 us; the launch traced here: 21.9 us
  Pallas kernels  20.6 us (94%)
  between operations  0.66 us (3%)
  local copies, waits for them, and re-layouts  0.6 us (3%)
    pallas_call x1, Pallas kernels, fused(): pl.pallas_call(functools.partial(window_kernel, n, m), out_shape=pltpu.VM...  20.6 us
    unnamed x1, local copies, waits for them, and re-layouts  0.6 us

profile of v4, /device:TPU:0, one launch (start us, length us, event | category | flops | bytes accessed | tf_op | source)
XLA Modules:
  0.0 21.9 jit_solution(7448295046298026567)
XLA Ops:
  0.7 20.6 %fused_window.1 = f32[16,128]{1,0:T(8,128)S(1)} custom-call(f32[1]{0:T(128)S(6)} %copy.12.guidance, bf16[32,2048]{1,0:T(8,128)(2,1)} %big_q.1, bf16[32,2048]{1,0:T(8,128)(2,1)} %big_k.1, bf16[32,2048]{1,0:T(8,128)(2,1)} %big_v.1, bf16[16,1024]{1,0:T(8,128)(2,1)} %small_q.1, bf16[16,1024]{1,0:T(8,128)(2,1)} %small_k.1, bf16[16,1024]{1,0:T(8,128)(2,1)} %small_v.1, ...), custom_call_target="tpu_custom_call" | custom-call | tf_op jit(solution)/shard_map/fused_window/pallas_call | solution.py:578
  21.3 0.6 %copy.11 = f32[16,128]{1,0:T(8,128)} copy(f32[16,128]{1,0:T(8,128)S(1)} %fused_window.1) | data formatting | bytes 16384

commit v5 on v4

--- a/solution.py
+++ b/solution.py
@@ -202,6 +202,7 @@
     latent,
     first_stage,
     stage,
+    first_arrived,
     arrived,
     swap,
     guide,
@@ -212,6 +213,7 @@
     value_sem,
     few_send,
     few_recv,
+    first_sem,
     back_sem,
     swap_sem,
 ):
@@ -312,6 +314,16 @@
             send_sem=back_sem.at[0],
             recv_sem=back_sem.at[1],
             device_id=(group, peer, which),
+            device_id_type=MESH,
+        )
+
+    def first_copy(which):
+        return pltpu.make_async_remote_copy(
+            src_ref=first_stage,
+            dst_ref=first_arrived.at[me * m + core],
+            send_sem=first_sem.at[0],
+            recv_sem=first_sem.at[1],
+            device_id=(group, 0, which),
             device_id_type=MESH,
         )
 
@@ -433,7 +445,7 @@
     guide_copy.wait()
     weight_value = guide[0]
 
-    def attend_rows(first, count, few_waits, head_waits):
+    def attend_rows(first, count, few_waits, query_waits):
         block = pl.ds(first, count)
         lanes = lax.broadcasted_iota(jnp.int32, (count, 2 * lat), 1)
 
@@ -448,21 +460,23 @@
             ]
             held = jnp.concatenate(sides, axis=1).reshape(tokens, 2 * lat)
             term = jnp.dot(probs, held.astype(few_w.dtype), preferred_element_type=jnp.float32)
-            small_part[block, :] = weight_value * term / totals
+            small_part[block, :] = jnp.where(lanes < lat, weight_value * term / totals, 0.0)
 
         @pl.when(core != host)
         def _():
             small_part[block, :] = jnp.zeros((count, 2 * lat), jnp.float32)
 
+        query_waits()
+        held = all_w[...]
+        parts = []
         for head in range(heads_here):
-            head_waits(head)
             columns = slice(head * DH, (head + 1) * DH)
             probs, totals = softmax_parts(all_q[block, columns], all_k[:, columns])
-            term = jnp.dot(probs, all_w[...], preferred_element_type=jnp.float32) / totals
-            term = (1.0 + weight_value) * term
-            if head == 0:
-                small_part[block, :] = term - small_part[block, :]
-        term = jnp.where(lanes < lat, small_part[block, :], term)
+            parts.append((jnp.dot(probs, held, preferred_element_type=jnp.float32), totals))
+        (left, left_totals), (right, right_totals) = parts
+        totals = jnp.where(lanes < lat, left_totals, right_totals)
+        term = (1.0 + weight_value) * (jnp.where(lanes < lat, left, right) / totals)
+        term = term - small_part[block, :]
         latent[block, :] = term + pltpu.roll(term, lat, 1)
         pair_rows = count // 2
         even = latent[pl.ds(first, pair_rows, stride=2), :]
@@ -477,18 +491,14 @@
     def later_few_waits():
         await_bytes(few_q.at[pl.ds(0, later), :], few_recv.at[3])
 
-    def first_head_waits(head):
-        if head == 0:
-            await_bytes(all_q.at[pl.ds(0, rows), :], big_recv.at[1])
-
-    def later_head_waits(head):
-        if head == 0:
-            await_bytes(all_q.at[pl.ds(0, later), :], big_recv.at[2])
+    def first_waits():
+        await_bytes(all_q.at[pl.ds(0, rows), :], big_recv.at[1])
+
+    def later_waits():
+        await_bytes(all_q.at[pl.ds(0, later), :], big_recv.at[2])
 
     def attend_first():
-        first_stage[...] = attend_rows(0, rows, first_few_waits, first_head_waits).reshape(
-            m, part, 2 * lat
-        )
+        first_stage[...] = attend_rows(0, rows, first_few_waits, first_waits)
 
     @pl.when(core == host)
     def _():
@@ -503,20 +513,18 @@
     def _():
         attend_first()
         for which in range(m):
-            back_copy(0, which, first_stage.at[which]).start()
-
-    stage[...] = attend_rows(rows, later, later_few_waits, later_head_waits).reshape(
+            first_copy(which).start()
+
+    stage[...] = attend_rows(rows, later, later_few_waits, later_waits).reshape(
         (n - 1) * m, part, 2 * lat
     )
 
     def start_back(peer):
-        @pl.when(peer != 0)
-        def _():
-            for which in range(m):
-                back_copy(peer, which, stage.at[(peer - 1) * m + which]).start()
-
-    for distance in range(rungs, 0, -1):
-        toward(distance, start_back)
+        for which in range(m):
+            back_copy(peer, which, stage.at[(peer - 1) * m + which]).start()
+
+    for peer in range(1, n):
+        pl.when(me != peer)(functools.partial(start_back, peer))
 
     @pl.when(me != 0)
     def _():
@@ -527,19 +535,28 @@
     @pl.when(me == 0)
     def _():
         attend_first()
-        arrived[core] = first_stage[core]
-        back_copy(0, 1 - core, first_stage.at[1 - core]).start()
-
-    everyone = arrived.at[pl.ds(0, n * m - 1)]
-    await_bytes(everyone, back_sem.at[1])
-    swap[0] = jnp.sum(arrived[...], axis=0)
-    swap_copy().start()
-    out[pl.ds(pl.multiple_of(core * part, part), part), :] = swap[0]
+        first_arrived[core] = first_stage[...]
+        first_copy(1 - core).start()
+
+    @pl.when(me == 0)
+    def _():
+        await_bytes(first_arrived.at[pl.ds(0, n * m - 1)], first_sem.at[1])
+        out[...] = jnp.sum(first_arrived[...], axis=0)
+        await_bytes(stage, back_sem.at[0])
+        await_bytes(first_stage, first_sem.at[0])
+
+    @pl.when(me != 0)
+    def _():
+        await_bytes(arrived.at[pl.ds(0, n * m - 1)], back_sem.at[1])
+        swap[0] = jnp.sum(arrived[...], axis=0)
+        swap_copy().start()
+        out[pl.ds(pl.multiple_of(core * part, part), part), :] = swap[0]
+        await_bytes(arrived.at[pl.ds(0, n * m - 1 - m)], back_sem.at[0])
+        await_bytes(first_arrived.at[pl.ds(0, m)], first_sem.at[0])
 
     await_bytes(all_k.at[pl.ds(0, later), :], big_send.at[0])
     await_bytes(all_q.at[pl.ds(0, later), :], big_send.at[1])
     await_bytes(all_w.at[pl.ds(0, later), :], value_sem.at[0])
-    await_bytes(everyone, back_sem.at[0])
 
     def await_few(chips):
         for item in (0, 2):
@@ -549,8 +566,10 @@
     pl.when(core == host)(functools.partial(await_few, n - 1))
     pl.when(core != host)(functools.partial(await_few, n))
 
-    swap_copy().wait()
-    out[pl.ds(pl.multiple_of((1 - core) * part, part), part), :] = swap[1]
+    @pl.when(me != 0)
+    def _():
+        swap_copy().wait()
+        out[pl.ds(pl.multiple_of((1 - core) * part, part), part), :] = swap[1]
 
 
 def fused(
@@ -595,8 +614,9 @@
             pltpu.VMEM((n, few_rows // 2, 2 * lat), kind),
             pltpu.VMEM((tokens, 2 * lat), jnp.float32),
             pltpu.VMEM((tokens, 2 * lat), jnp.float32),
-            pltpu.VMEM((m, part, 2 * lat), jnp.float32),
+            pltpu.VMEM((half, 2 * lat), jnp.float32),
             pltpu.VMEM(((n - 1) * m, part, 2 * lat), jnp.float32),
+            pltpu.VMEM((n * m, half, 2 * lat), jnp.float32),
             pltpu.VMEM((n * m, part, 2 * lat), jnp.float32),
             pltpu.VMEM((2, part, 2 * lat), jnp.float32),
             pltpu.SMEM((1,), jnp.float32),
@@ -607,6 +627,7 @@
             dma((2,)),
             dma((3,)),
             dma((4,)),
+            dma((2,)),
             dma((2,)),
             dma((2,)),
         ],

time: 22 us -> 21.8 us (level)
  the two profiles are of different devices: /device:TPU:0 before, /device:TPU:3 now
where the time goes in v5:
time: 21.8 us; the launch traced here: 21.7 us
  Pallas kernels  20.4 us (94%)
  between operations  0.66 us (3%)
  local copies, waits for them, and re-layouts  0.6 us (3%)
    pallas_call x1, Pallas kernels, fused(): pl.pallas_call(functools.partial(window_kernel, n, m), out_shape=pltpu.VM...  20.4 us
    unnamed x1, local copies, waits for them, and re-layouts  0.6 us

profile of v5, /device:TPU:3, one launch (start us, length us, event | category | flops | bytes accessed | tf_op | source)
XLA Modules:
  0.0 21.7 jit_solution(14777972913091188241)
XLA Ops:
  0.7 20.4 %fused_window.1 = f32[16,128]{1,0:T(8,128)S(1)} custom-call(f32[1]{0:T(128)S(6)} %copy.12.guidance, bf16[32,2048]{1,0:T(8,128)(2,1)} %big_q.1, bf16[32,2048]{1,0:T(8,128)(2,1)} %big_k.1, bf16[32,2048]{1,0:T(8,128)(2,1)} %big_v.1, bf16[16,1024]{1,0:T(8,128)(2,1)} %small_q.1, bf16[16,1024]{1,0:T(8,128)(2,1)} %small_k.1, bf16[16,1024]{1,0:T(8,128)(2,1)} %small_v.1, ...), custom_call_target="tpu_custom_call" | custom-call | tf_op jit(solution)/shard_map/fused_window/pallas_call | solution.py:597
  21.1 0.6 %copy.11 = f32[16,128]{1,0:T(8,128)} copy(f32[16,128]{1,0:T(8,128)S(1)} %fused_window.1) | data formatting | bytes 16384

commit v6 on v5

--- a/solution.py
+++ b/solution.py
@@ -431,10 +431,8 @@
             toward(distance, start_early, True)
             toward(distance, start_early, False)
         held, known = known, reach
-    for distance in range(held + 1, rungs + 1):
-        toward(distance, start_late)
-    for distance in range(held, 0, -1):
-        toward(distance, start_late)
+    for peer in range(n - 1, -1, -1):
+        pl.when(me != peer)(functools.partial(start_late, peer))
 
     @pl.when(core != host)
     def _():

time: 21.8 us -> 21.8 us (level)
  no operation moved by 1% of the time
where the time goes in v6:
time: 21.8 us; the launch traced here: 21.7 us
  Pallas kernels  20.4 us (94%)
  between operations  0.66 us (3%)
  local copies, waits for them, and re-layouts  0.6 us (3%)
    pallas_call x1, Pallas kernels, fused(): pl.pallas_call(functools.partial(window_kernel, n, m), out_shape=pltpu.VM...  20.4 us
    unnamed x1, local copies, waits for them, and re-layouts  0.6 us

profile of v6, /device:TPU:3, one launch (start us, length us, event | category | flops | bytes accessed | tf_op | source)
XLA Modules:
  0.0 21.7 jit_solution(17907693965898557966)
XLA Ops:
  0.7 20.4 %fused_window.1 = f32[16,128]{1,0:T(8,128)S(1)} custom-call(f32[1]{0:T(128)S(6)} %copy.12.guidance, bf16[32,2048]{1,0:T(8,128)(2,1)} %big_q.1, bf16[32,2048]{1,0:T(8,128)(2,1)} %big_k.1, bf16[32,2048]{1,0:T(8,128)(2,1)} %big_v.1, bf16[16,1024]{1,0:T(8,128)(2,1)} %small_q.1, bf16[16,1024]{1,0:T(8,128)(2,1)} %small_k.1, bf16[16,1024]{1,0:T(8,128)(2,1)} %small_v.1, ...), custom_call_target="tpu_custom_call" | custom-call | tf_op jit(solution)/shard_map/fused_window/pallas_call | solution.py:595
  21.1 0.6 %copy.11 = f32[16,128]{1,0:T(8,128)} copy(f32[16,128]{1,0:T(8,128)S(1)} %fused_window.1) | data formatting | bytes 16384
